TPU v7x, 32 devices: a whole 2x2x4 slice. The times are simulated.
32 devices in a mesh: grp: 4 (over y, x), dev: 8 (over z, core).
Axes of the slice: x: 2, y: 2, z: 4, core: 2. Of those that a mesh axis runs over, the one named last changes fastest.
Arguments:
- tokens: bfloat16 [8192, 1024], P(('grp', 'dev')), may hold values from -6 to 6
- cotangent: bfloat16 [8192, 1024], P(('grp', 'dev')), may hold values from -6 to 6
- lengths: int32 [8], replicated, may hold values from 256 to 1024, as said below
- offsets: int32 [8], replicated, may hold values from 0 to 768, as said below
- ln_gain: bfloat16 [1024], P(('grp', 'dev')), may hold values from 0.5 to 1.5
- ln_bias: bfloat16 [1024], P(('grp', 'dev')), may hold values from -2 to 2
- w_qkv: bfloat16 [1024, 3072], P(('grp', 'dev')), may hold values from -0.1875 to 0.1875
- w_out: bfloat16 [1024, 1024], P(('grp', 'dev')), may hold values from -3 to 3
- w_fc1: bfloat16 [1024, 4096], P(('grp', 'dev')), may hold values from -0.1875 to 0.1875
- b_fc1: bfloat16 [4096], P(('grp', 'dev')), may hold values from -2 to 2
- w_fc2: bfloat16 [4096, 1024], P(('grp', 'dev')), may hold values from -0.09375 to 0.09375
- b_fc2: bfloat16 [1024], P(('grp', 'dev')), may hold values from -2 to 2
Outputs:
- mixed: bfloat16 [8192, 1024], P(('grp', 'dev'))
- token_grad: bfloat16 [8192, 1024], P(('grp', 'dev'))
- g_ln_gain: float32 [1024], P('dev')
- g_ln_bias: float32 [1024], P('dev')
- g_w_qkv: float32 [1024, 3072], P('dev')
- g_w_out: float32 [1024, 1024], P('dev')
- g_w_fc1: float32 [1024, 4096], P('dev')
- g_b_fc1: float32 [4096], P('dev')
- g_w_fc2: float32 [4096, 1024], P('dev')
- g_b_fc2: float32 [1024], P('dev')
Inputs may be any that keep to these rules, and one draw needn't show every extreme that they name: `lengths`: one slot in every draw has length 1024 and one has 256. offsets + lengths <= 1024; one slot of length 256 ends at place 1024 - 1.
All inputs are finite; a program needn't handle non-finite values.
Results may differ from a plain program's by a relative error of at most 0.015.
Values may be sent and summed in bfloat16 or wider, within the bound.
A program may use at most 192 MiB of HBM per device.

v0:
```python
import math

import jax
import jax.numpy as jnp
from jax import lax
from jax.sharding import PartitionSpec as P

HEADS = 16
ROT = 32
DPS = 4


def swapped(array, axis, distance):
    return lax.ppermute(array, axis, [(i, i ^ 1 << distance) for i in range(lax.axis_size(axis))])


def gelu_tanh(values_in):
    return (
        0.5
        * values_in
        * (
            1.0
            + jnp.tanh(
                0.7978845608028654 * (values_in + 0.044715 * values_in * values_in * values_in)
            )
        )
    )


def gelu_slope(values_in):
    tangent = jnp.tanh(
        0.7978845608028654 * (values_in + 0.044715 * values_in * values_in * values_in)
    )
    inner_slope = 0.7978845608028654 * (1.0 + 0.134145 * values_in * values_in)
    return 0.5 * (1.0 + tangent) + 0.5 * values_in * (1.0 - tangent * tangent) * inner_slope


def turn_tables(places):
    half_rot = ROT // 2
    frequency = jnp.exp(jnp.arange(half_rot, dtype=jnp.float32) * (-2.0 * math.log(10000.0) / ROT))
    angles = places[:, None] * frequency[None, :]
    return (jnp.cos(angles)[:, None, :], jnp.sin(angles)[:, None, :])


def rotate(field_in, cosine, sine_table):
    half_rot = ROT // 2
    first_half = field_in[..., :half_rot]
    second = field_in[..., half_rot:ROT]
    return jnp.concatenate(
        [
            first_half * cosine - second * sine_table,
            second * cosine + first_half * sine_table,
            field_in[..., ROT:],
        ],
        axis=-1,
    )


def rotate_back(field_in, cosine, sine_table):
    half_rot = ROT // 2
    first_half = field_in[..., :half_rot]
    second = field_in[..., half_rot:ROT]
    return jnp.concatenate(
        [
            first_half * cosine + second * sine_table,
            second * cosine - first_half * sine_table,
            field_in[..., ROT:],
        ],
        axis=-1,
    )


def place_of(local_rows, row_count, slot_len):
    piece = local_rows // row_count
    inner = local_rows % row_count
    half_rows = row_count // 2
    return jnp.where(
        inner < half_rows,
        piece * half_rows + inner,
        slot_len - (piece + 1) * half_rows + (inner - half_rows),
    )


def allowed_table(query_places, key_places, offset, length):
    live_keys = (key_places >= offset) & (key_places < offset + length)
    return (key_places[None, :] <= query_places[:, None]) & (
        live_keys[None, :] | (key_places[None, :] == query_places[:, None])
    )


def attend_forward(queries, key_stack, value_stack, allowed):
    head_size = queries.shape[2]
    score_scale = 1.0 / math.sqrt(head_size)
    head_group = math.gcd(HEADS, 4)
    outputs = []
    maxima = []
    for first_head in range(0, HEADS, head_group):
        part_query = queries[:, first_head : first_head + head_group]
        part_keys = key_stack[:, first_head : first_head + head_group]
        part_values = value_stack[:, first_head : first_head + head_group]
        scores = (
            jnp.einsum("qhd,khd->hqk", part_query, part_keys, preferred_element_type=jnp.float32)
            * score_scale
        )
        scores = jnp.where(allowed[None], scores, -1e30)
        row_max = jnp.max(scores, axis=-1, keepdims=True)
        expo = jnp.exp(scores - row_max)
        denom = jnp.sum(expo, axis=-1, keepdims=True)
        probs_low = (expo / denom).astype(jnp.bfloat16)
        outputs.append(
            jnp.einsum("hqk,khd->qhd", probs_low, part_values, preferred_element_type=jnp.float32)
        )
        maxima.append((row_max + jnp.log(denom))[..., 0])
    return (jnp.concatenate(outputs, axis=1), jnp.concatenate(maxima, axis=0))


def attend_backward(queries, key_stack, value_stack, grad_att, log_total, allowed):
    head_size = queries.shape[2]
    score_scale = 1.0 / math.sqrt(head_size)
    head_group = math.gcd(HEADS, 4)
    grad_q_parts = []
    grad_k_parts = []
    grad_v_parts = []
    for first_head in range(0, HEADS, head_group):
        part_query = queries[:, first_head : first_head + head_group]
        part_keys = key_stack[:, first_head : first_head + head_group]
        part_values = value_stack[:, first_head : first_head + head_group]
        part_grad = grad_att[:, first_head : first_head + head_group]
        part_total = log_total[first_head : first_head + head_group]
        scores = (
            jnp.einsum("qhd,khd->hqk", part_query, part_keys, preferred_element_type=jnp.float32)
            * score_scale
        )
        scores = jnp.where(allowed[None], scores, -1e30)
        probs = jnp.exp(scores - part_total[:, :, None])
        probs_low = probs.astype(jnp.bfloat16)
        grad_v_parts.append(
            jnp.einsum("hqk,qhd->khd", probs_low, part_grad, preferred_element_type=jnp.float32)
        )
        grad_prob = jnp.einsum(
            "qhd,khd->hqk", part_grad, part_values, preferred_element_type=jnp.float32
        )
        row_dot = jnp.sum(probs * grad_prob, axis=-1, keepdims=True)
        grad_score = (probs * (grad_prob - row_dot)).astype(jnp.bfloat16)
        grad_q_parts.append(
            jnp.einsum("hqk,khd->qhd", grad_score, part_keys, preferred_element_type=jnp.float32)
            * score_scale
        )
        grad_k_parts.append(
            jnp.einsum("hqk,qhd->khd", grad_score, part_query, preferred_element_type=jnp.float32)
            * score_scale
        )
    return (
        jnp.concatenate(grad_q_parts, axis=1),
        jnp.concatenate(grad_k_parts, axis=1),
        jnp.concatenate(grad_v_parts, axis=1),
    )


def local(
    tokens, cotangent, lengths, offsets, ln_gain, ln_bias, w_qkv, w_out, w_fc1, b_fc1, w_fc2, b_fc2
):
    row_count = tokens.shape[0]
    width = tokens.shape[1]
    head_size = width // HEADS
    slot_len = row_count * DPS
    bit_count = DPS.bit_length() - 1
    dev_count = lax.axis_size("dev")
    dev_index = lax.axis_index("dev")
    first_row = (lax.axis_index("grp") * dev_count + dev_index) * row_count
    slot_index = first_row // slot_len
    slot_piece = first_row % slot_len // row_count
    length = lengths[slot_index]
    offset = offsets[slot_index]
    query_places = place_of(
        slot_piece * row_count + jnp.arange(row_count, dtype=jnp.int32), row_count, slot_len
    )
    key_places = place_of(jnp.arange(slot_len, dtype=jnp.int32), row_count, slot_len)
    live_rows = (query_places >= offset) & (query_places < offset + length)
    live_float = live_rows.astype(jnp.float32)[:, None]
    cosine, sine_table = turn_tables((query_places - offset).astype(jnp.float32))
    allowed = allowed_table(query_places, key_places, offset, length)
    gathered = (
        lax.all_gather(ln_gain, ("grp", "dev"), axis=0, tiled=True),
        lax.all_gather(ln_bias, ("grp", "dev"), axis=0, tiled=True),
        lax.all_gather(w_qkv, ("grp", "dev"), axis=0, tiled=True),
        lax.all_gather(w_out, ("grp", "dev"), axis=0, tiled=True),
        lax.all_gather(w_fc1, ("grp", "dev"), axis=0, tiled=True),
        lax.all_gather(b_fc1, ("grp", "dev"), axis=0, tiled=True),
        lax.all_gather(w_fc2, ("grp", "dev"), axis=0, tiled=True),
        lax.all_gather(b_fc2, ("grp", "dev"), axis=0, tiled=True),
    )
    full_gain, full_bias, full_qkv, full_out, full_fc1, full_bfc1, full_fc2, full_bfc2 = gathered
    norm_gain = full_gain.astype(jnp.float32)
    tokens_f = tokens.astype(jnp.float32)
    centred = tokens_f - jnp.mean(tokens_f, axis=-1, keepdims=True)
    inverse = lax.rsqrt(jnp.mean(centred * centred, axis=-1, keepdims=True) + 1e-05)
    normed = centred * inverse
    hidden_low = (normed * norm_gain + full_bias.astype(jnp.float32)).astype(jnp.bfloat16)
    mixed_qkv = jnp.dot(hidden_low, full_qkv, preferred_element_type=jnp.float32)
    queries = rotate(
        mixed_qkv[:, :width].reshape(row_count, HEADS, head_size), cosine, sine_table
    ).astype(jnp.bfloat16)
    key_rows = rotate(
        mixed_qkv[:, width : 2 * width].reshape(row_count, HEADS, head_size), cosine, sine_table
    ).astype(jnp.bfloat16)
    value_rows = mixed_qkv[:, 2 * width :].astype(jnp.bfloat16)
    blocks = jnp.stack([key_rows.reshape(row_count, width), value_rows])[:, None]
    for bit in range(bit_count):
        partner = swapped(blocks, "dev", bit)
        upper = dev_index // (1 << bit) % 2 == 1
        blocks = jnp.where(
            upper,
            jnp.concatenate([partner, blocks], axis=1),
            jnp.concatenate([blocks, partner], axis=1),
        )
    key_stack = blocks[0].reshape(slot_len, HEADS, head_size)
    value_stack = blocks[1].reshape(slot_len, HEADS, head_size)
    attended, log_total = attend_forward(queries, key_stack, value_stack, allowed)
    attended_low = attended.reshape(row_count, width).astype(jnp.bfloat16)
    pre_act = jnp.dot(hidden_low, full_fc1, preferred_element_type=jnp.float32) + full_bfc1.astype(
        jnp.float32
    )
    act_low = gelu_tanh(pre_act).astype(jnp.bfloat16)
    attn_part = jnp.dot(attended_low, full_out, preferred_element_type=jnp.float32)
    mlp_part = jnp.dot(act_low, full_fc2, preferred_element_type=jnp.float32) + full_bfc2.astype(
        jnp.float32
    )
    mixed = (live_float * (tokens_f + attn_part + mlp_part)).astype(jnp.bfloat16)
    back_gain, back_qkv, back_out, back_fc1, back_fc2 = (
        lax.all_gather(ln_gain, ("grp", "dev"), axis=0, tiled=True),
        lax.all_gather(w_qkv, ("grp", "dev"), axis=0, tiled=True),
        lax.all_gather(w_out, ("grp", "dev"), axis=0, tiled=True),
        lax.all_gather(w_fc1, ("grp", "dev"), axis=0, tiled=True),
        lax.all_gather(w_fc2, ("grp", "dev"), axis=0, tiled=True),
    )
    back_gain = back_gain.astype(jnp.float32)
    grad_y = cotangent.astype(jnp.float32) * live_float
    grad_low = grad_y.astype(jnp.bfloat16)
    g_w_out = jnp.einsum("rd,re->de", attended_low, grad_low, preferred_element_type=jnp.float32)
    g_b_fc2 = jnp.sum(grad_y, axis=0)
    g_w_fc2 = jnp.einsum("rf,re->fe", act_low, grad_low, preferred_element_type=jnp.float32)
    grad_act = jnp.einsum("re,fe->rf", grad_low, back_fc2, preferred_element_type=jnp.float32)
    grad_pre = (grad_act * gelu_slope(pre_act)).astype(jnp.bfloat16)
    g_w_fc1 = jnp.einsum("rd,rf->df", hidden_low, grad_pre, preferred_element_type=jnp.float32)
    g_b_fc1 = jnp.sum(grad_pre.astype(jnp.float32), axis=0)
    grad_h = jnp.einsum("rf,df->rd", grad_pre, back_fc1, preferred_element_type=jnp.float32)
    grad_att = jnp.einsum(
        "re,de->rd", grad_low, back_out, preferred_element_type=jnp.float32
    ).astype(jnp.bfloat16)
    grad_query, grad_keys, grad_values = attend_backward(
        queries,
        key_stack,
        value_stack,
        grad_att.reshape(row_count, HEADS, head_size),
        log_total,
        allowed,
    )
    back_blocks = jnp.stack(
        [grad_keys.reshape(slot_len, width), grad_values.reshape(slot_len, width)]
    ).reshape(2, DPS, row_count, width)
    for bit in range(bit_count - 1, -1, -1):
        count_now = back_blocks.shape[1] // 2
        lower_half = back_blocks[:, :count_now]
        upper_half = back_blocks[:, count_now:]
        upper = dev_index // (1 << bit) % 2 == 1
        kept = jnp.where(upper, upper_half, lower_half)
        outgoing = jnp.where(upper, lower_half, upper_half)
        back_blocks = kept + swapped(outgoing, "dev", bit)
    own_keys = back_blocks[0, 0]
    own_values = back_blocks[1, 0]
    grad_q_pre = rotate_back(grad_query, cosine, sine_table).reshape(row_count, width)
    grad_k_pre = rotate_back(
        own_keys.reshape(row_count, HEADS, head_size), cosine, sine_table
    ).reshape(row_count, width)
    grad_qkv = jnp.concatenate([grad_q_pre, grad_k_pre, own_values], axis=1).astype(jnp.bfloat16)
    g_w_qkv = jnp.einsum("rd,re->de", hidden_low, grad_qkv, preferred_element_type=jnp.float32)
    grad_h = grad_h + jnp.einsum(
        "re,de->rd", grad_qkv, back_qkv, preferred_element_type=jnp.float32
    )
    g_ln_gain = jnp.sum(grad_h * normed, axis=0)
    g_ln_bias = jnp.sum(grad_h, axis=0)
    scaled_grad = grad_h * back_gain
    grad_norm = inverse * (
        scaled_grad
        - jnp.mean(scaled_grad, axis=-1, keepdims=True)
        - normed * jnp.mean(scaled_grad * normed, axis=-1, keepdims=True)
    )
    token_grad = (grad_y + grad_norm).astype(jnp.bfloat16)
    gradients = (g_ln_gain, g_ln_bias, g_w_qkv, g_w_out, g_w_fc1, g_b_fc1, g_w_fc2, g_b_fc2)
    shares = (
        lax.psum_scatter(
            gradients[0].astype(jnp.bfloat16), "dev", scatter_dimension=0, tiled=True
        ).astype(jnp.float32),
        lax.psum_scatter(
            gradients[1].astype(jnp.bfloat16), "dev", scatter_dimension=0, tiled=True
        ).astype(jnp.float32),
        lax.psum_scatter(
            gradients[2].astype(jnp.bfloat16), "dev", scatter_dimension=0, tiled=True
        ).astype(jnp.float32),
        lax.psum_scatter(
            gradients[3].astype(jnp.bfloat16), "dev", scatter_dimension=0, tiled=True
        ).astype(jnp.float32),
        lax.psum_scatter(
            gradients[4].astype(jnp.bfloat16), "dev", scatter_dimension=0, tiled=True
        ).astype(jnp.float32),
        lax.psum_scatter(
            gradients[5].astype(jnp.bfloat16), "dev", scatter_dimension=0, tiled=True
        ).astype(jnp.float32),
        lax.psum_scatter(
            gradients[6].astype(jnp.bfloat16), "dev", scatter_dimension=0, tiled=True
        ).astype(jnp.float32),
        lax.psum_scatter(
            gradients[7].astype(jnp.bfloat16), "dev", scatter_dimension=0, tiled=True
        ).astype(jnp.float32),
    )
    summed = (
        lax.psum(shares[0].astype(jnp.bfloat16), "grp").astype(jnp.float32),
        lax.psum(shares[1].astype(jnp.bfloat16), "grp").astype(jnp.float32),
        lax.psum(shares[2].astype(jnp.bfloat16), "grp").astype(jnp.float32),
        lax.psum(shares[3].astype(jnp.bfloat16), "grp").astype(jnp.float32),
        lax.psum(shares[4].astype(jnp.bfloat16), "grp").astype(jnp.float32),
        lax.psum(shares[5].astype(jnp.bfloat16), "grp").astype(jnp.float32),
        lax.psum(shares[6].astype(jnp.bfloat16), "grp").astype(jnp.float32),
        lax.psum(shares[7].astype(jnp.bfloat16), "grp").astype(jnp.float32),
    )
    return (mixed, token_grad) + tuple(summed)


def solution(mesh):
    return jax.shard_map(
        local,
        mesh=mesh,
        in_specs=(
            P(("grp", "dev"), None),
            P(("grp", "dev"), None),
            P(),
            P(),
            P(("grp", "dev")),
            P(("grp", "dev")),
            P(("grp", "dev"), None),
            P(("grp", "dev"), None),
            P(("grp", "dev"), None),
            P(("grp", "dev")),
            P(("grp", "dev"), None),
            P(("grp", "dev")),
        ),
        out_specs=(
            P(("grp", "dev"), None),
            P(("grp", "dev"), None),
            P("dev"),
            P("dev"),
            P("dev", None),
            P("dev", None),
            P("dev", None),
            P("dev"),
            P("dev", None),
            P("dev"),
        ),
        check_vma=False,
    )
```

profile of v0, /device:TPU:9, one launch (start us, length us, event | category | flops | bytes accessed | tf_op | source)
XLA Modules:
  0.0 790.5 jit_solution(6765322636481741186)
XLA Ops:
  12.6 40.6 %all-reduce.7 = (bf16[1024]{0:T(1024)(128)(2,1)}, bf16[1024]{0:T(1024)(128)(2,1)S(1)}, bf16[1024]{0:T(1024)(128)(2,1)S(1)}) all-reduce(bf16[1024]{0:T(1024)(128)(2,1)S(1)} %dynamic-update-slice.2, bf16[1024]{0:T(1024)(128)(2,1)S(1)} %dynamic-update-slice.1, ...), channel_id=1, replica_groups=mesh['grp'=4,'dev'=8] {'grp','dev'}, use_global_device_ids=true, to_apply=%add.2 | all-reduce | flops 3072 | bytes 12288
  59.0 23.1 %all-gather.6.cloned.1.call-done = bf16[1024,3072]{1,0:T(8,128)(2,1)} async-done(((bf16[32,3072]{1,0:T(8,128)(2,1)}), bf16[1024,3072]{1,0:T(8,128)(2,1)}) %all-gather.6.cloned.1.call-update) | async-done | bytes 6291472 | tf_op jit(solution)/shard_map/all_gather | solution.py:186
  82.1 4.9 fusion.118
  93.0 2.5 collective-permute-done
  95.5 1.9 maximum_select_fusion.1
  102.5 77.0 %collective-permute-done.1 = bf16[2,2,256,1024]{3,2,0,1:T(8,128)(2,1)} collective-permute-done((bf16[2,2,256,1024]{3,2,0,1:T(8,128)(2,1)S(1)}, bf16[2,2,256,1024]{3,2,0,1:T(8,128)(2,1)}, u32[]{:S(2)}, u32[]{:S(2)}) %collective-permute-start.1) | collective-permute-done | bytes 2097184 | tf_op jit(solution)/shard_map/ppermute | solution.py:14
  179.5 2.6 maximum_select_fusion
  182.1 2.4 fusion.120
  184.5 3.0 copy.55
  187.6 2.7 reshape_squeeze.10
  190.3 3.1 copy.53
  193.4 2.9 reshape_squeeze.9
  196.3 2.1 fusion.122
  199.5 2.0 copy-done.27
  208.2 2.0 copy-done.18
  215.4 2.2 convolution_convert_fusion.3
  217.6 40.0 %all-gather = bf16[32,1,128]{2,1,0:T(2,128)(2,1)S(1)} all-gather(bf16[1,1,128]{2,1,0:T(2,128)(2,1)} %bitcast.117), channel_id=1, replica_groups=mesh['grp'=4,'dev'=8] {'grp','dev'}, dimensions={0}, use_global_device_ids=true | all-gather | bytes 8448 | tf_op jit(solution)/shard_map/all_gather | solution.py:189
  258.3 5.9 convolution_add_fusion
  264.1 2.0 copy-done.63
  266.1 5.5 convolution_convert_fusion
  271.7 3.1 convolution_convert_fusion.4
  278.2 4.0 fusion.40
  282.2 38.2 %all-gather.12.cloned.1.call-done = bf16[4096,1024]{1,0:T(8,128)(2,1)} async-done(((bf16[128,1024]{1,0:T(8,128)(2,1)}), bf16[4096,1024]{1,0:T(8,128)(2,1)}) %all-gather.12.cloned.1.call-update) | async-done | bytes 8388624 | tf_op jit(solution)/shard_map/all_gather | solution.py:190
  320.4 8.2 %fusion.126 = (bf16[4096]{0:T(1024)(128)(2,1)}, bf16[256,4096]{1,0:T(8,128)(2,1)S(1)}) fusion(f32[256,4096]{1,0:T(8,128)} %copy-done.63, bf16[4096,1024]{1,0:T(8,128)(2,1)} %all-gather.12.cloned.1.call-done, bf16[256,1024]{1,0:T(8,128)(2,1)} %param.13, f32[256]{0:T(256)} %copy-done.41), kind=kOutput, calls=%fused_computation.212 | convolution fusion | flops 2169237504 | bytes 15213568 | tf_op jit(solution)/shard_map/re,fe->rf/dot_general | solution.py:243
  330.0 5.8 convolution_convert_fusion.1
  336.7 3.3 fusion.37
  343.4 2.6 pad_maximum_fusion.1
  346.0 5.8 stack.16
  351.8 3.8 multiply_reduce_fusion
  358.6 1.6 multiply_reduce_fusion.1
  363.1 1.6 multiply_reduce_fusion.3
  366.1 1.6 copy-done.2
  372.0 2.5 pad_maximum_fusion
  374.5 5.8 stack.15
  380.3 3.2 copy_dynamic-update-slice_fusion.1
  385.9 168.4 %collective-permute-done.2 = f32[2,2,256,1024]{2,3,1,0:T(8,128)S(1)} collective-permute-done((f32[2,2,256,1024]{2,3,1,0:T(8,128)S(1)}, f32[2,2,256,1024]{2,3,1,0:T(8,128)S(1)}, u32[]{:S(2)}, u32[]{:S(2)}) %collective-permute-start.2) | collective-permute-done | bytes 4194336 | tf_op jit(solution)/shard_map/ppermute | solution.py:14
  562.7 4.6 convolution_convert_fusion.2
  569.9 33.8 %reduce-scatter.9.cloned.1.call-done = bf16[128,4096]{1,0:T(8,128)(2,1)} async-done(((bf16[1024,4096]{1,0:T(8,128)(2,1)}), bf16[128,4096]{1,0:T(8,128)(2,1)}) %reduce-scatter.9.cloned.1.call-update) | async-done | bytes 1048592 | tf_op jit(solution)/shard_map/reduce_scatter | solution.py:304
  603.7 81.2 %reduce-scatter.5.cloned.1.call-done = bf16[128,3072]{1,0:T(8,128)(2,1)} async-done(((bf16[1024,3072]{1,0:T(8,128)(2,1)}), bf16[128,3072]{1,0:T(8,128)(2,1)}) %reduce-scatter.5.cloned.1.call-update) | async-done | bytes 786448 | tf_op jit(solution)/shard_map/reduce_scatter | solution.py:298
  685.0 7.5 convolution_add_fusion.2
  694.2 6.1 fusion.127
  700.3 5.2 fusion.75
  706.8 21.8 %all-reduce.8 = (bf16[1024]{0:T(1024)(128)(2,1)S(1)}, bf16[1024]{0:T(1024)(128)(2,1)S(1)}, bf16[4096]{0:T(1024)(128)(2,1)S(1)}, bf16[1024]{0:T(1024)(128)(2,1)S(1)}) all-reduce(bf16[1024]{0:T(1024)(128)(2,1)S(1)} %get-tuple-element.10, bf16[1024]{0:T(1024)(128)(2,1)S(1)} %get-tuple-element.13, ...), channel_id=2, replica_groups=mesh['grp'=4,'dev'=8] {'dev'}, use_global_device_ids=true, to_apply=%region_17.18.clone | all-reduce | flops 7168 | bytes 28672
  728.9 8.2 %all-reduce.9 = (bf16[128]{0:T(256)(128)(2,1)S(1)}, bf16[128]{0:T(256)(128)(2,1)S(1)}, bf16[512]{0:T(512)(128)(2,1)S(1)}, bf16[128]{0:T(256)(128)(2,1)S(1)}) all-reduce(bf16[128]{0:T(256)(128)(2,1)S(1)} %dynamic-slice.1, bf16[128]{0:T(256)(128)(2,1)S(1)} %dynamic-slice.3, ...), channel_id=1, replica_groups=mesh['grp'=4,'dev'=8] {'grp'}, use_global_device_ids=true, to_apply=%region_18.19 | all-reduce | flops 896 | bytes 3584 | tf_op jit(solution)/shard_map/psum | solution.py:318
  739.2 35.7 %all-reduce.13.cloned.1.call-done = (bf16[128,3072]{1,0:T(8,128)(2,1)}, bf16[128,1024]{1,0:T(8,128)(2,1)}, bf16[128,4096]{1,0:T(8,128)(2,1)}, bf16[512,1024]{1,0:T(8,128)(2,1)}) async-done(((bf16[128,3072]{1,0:T(8,128)(2,1)}, bf16[128,1024]{1,0:T(8,128)(2,1)}, bf16[128,4096]{1,0:T(8,128)(2,1)}, bf16[512,1024]{1,0:T(8,128)(2,1)}), (bf16[128,3072]{1,0:T(8,128)(2,1)}, bf16[128,1024]{1,0:T(8,128)(2,1)}, ...) | async-done | bytes 3145744 | tf_op jit(solution)/shard_map/psum | solution.py:320
  774.9 1.9 convert_element_type.207
  776.8 2.4 convert_element_type.205
  779.2 2.8 convert_element_type.209
  (243 shorter events, 73.3 us)
Async XLA Ops:
  7.2 74.9 %all-gather.6.cloned.1.call-start = ((), (), s32[]{:S(2)}) async-start(), calls=%async_computation.4 | async-start | bytes 6488064 | tf_op jit(solution)/shard_map/all_gather | solution.py:186
  7.9 250.3 %all-gather.10.cloned.1.call-start = ((), (), s32[]{:S(2)}) async-start(), calls=%async_computation.6 | async-start | bytes 8650752 | tf_op jit(solution)/shard_map/all_gather | solution.py:188
  8.7 263.0 %all-gather.8.cloned.1.call-start = ((), (), s32[]{:S(2)}) async-start(), calls=%async_computation.5 | async-start | bytes 2162688 | tf_op jit(solution)/shard_map/all_gather | solution.py:187
  9.4 311.0 %all-gather.12.cloned.1.call-start = ((), (), s32[]{:S(2)}) async-start(), calls=%async_computation.7 | async-start | bytes 8650752 | tf_op jit(solution)/shard_map/all_gather | solution.py:190
  10.0 559.9 %reduce-scatter.7.cloned.1.call-start = ((), (), s32[]{:S(2)}) async-start(), calls=%async_computation.9 | async-start | bytes 2359296 | tf_op jit(solution)/shard_map/reduce_scatter | solution.py:301
  56.9 201.3 %copy-start.43 = (f32[256]{0:T(256)}, f32[256]{0:T(256)S(1)}, u32[]{:S(2)}) copy-start(f32[256]{0:T(256)S(1)} %broadcast_multiply_fusion.2) | copy-start | bytes 3076
  58.3 28.7 %copy-start.46 = (f32[256]{0:T(256)}, f32[256]{0:T(256)S(1)}, u32[]{:S(2)}) copy-start(f32[256]{0:T(256)S(1)} %add_rsqrt_fusion) | copy-start | bytes 3076
  90.9 6.9 copy-start.61
  91.0 10.1 %copy-start.59 = (s32[256]{0:T(256)S(1)}, s32[256]{0:T(256)}, u32[]{:S(2)}) copy-start(s32[256]{0:T(256)} %get-tuple-element.68) | copy-start | bytes 3076
  92.6 2.9 collective-permute-start
  97.4 82.1 %collective-permute-start.1 = (bf16[2,2,256,1024]{3,2,0,1:T(8,128)(2,1)S(1)}, bf16[2,2,256,1024]{3,2,0,1:T(8,128)(2,1)}, u32[]{:S(2)}, u32[]{:S(2)}) collective-permute-start(bf16[2,2,256,1024]{3,2,0,1:T(8,128)(2,1)S(1)} %maximum_select_fusion.1), channel_id=1, source_target_pairs={{0,2},{1,3},{2,0},{3,1},{4,6},{5,7},{6,4},{7,5},{8,10},{9,11},{10,... | collective-permute-start | bytes 6291464 | tf_op jit(solution)/shard_map/ppermute | solution.py:14
  100.4 171.3 %copy-start.41 = (f32[256]{0:T(256)}, f32[256]{0:T(256)S(1)}, u32[]{:S(2)}) copy-start(f32[256]{0:T(256)S(1)} %and_convert_fusion) | copy-start | bytes 3076
  190.3 6.0 copy-start.23
  198.5 9.7 %copy-start.8 = (f32[4,256,1024]{2,1,0:T(8,128)}, f32[4,256,1024]{2,1,0:T(8,128)S(1)}, u32[]{:S(2)}) copy-start(f32[4,256,1024]{2,1,0:T(8,128)S(1)} %get-tuple-element.50) | copy-start | bytes 12582916
  198.5 9.7 %copy-start.51 = (f32[4,256]{1,0:T(4,128)}, f32[4,256]{1,0:T(4,128)S(1)}, u32[]{:S(2)}) copy-start(f32[4,256]{1,0:T(4,128)S(1)} %get-tuple-element.49) | copy-start | bytes 12292
  201.6 6.6 copy-start.53
  202.7 8.6 %copy-start.3 = (f32[4,256,1024]{2,1,0:T(8,128)}, f32[4,256,1024]{2,1,0:T(8,128)S(1)}, u32[]{:S(2)}) copy-start(f32[4,256,1024]{2,1,0:T(8,128)S(1)} %get-tuple-element.52) | copy-start | bytes 12582916
  202.7 8.6 %copy-start.54 = (f32[4,256]{1,0:T(4,128)}, f32[4,256]{1,0:T(4,128)S(1)}, u32[]{:S(2)}) copy-start(f32[4,256]{1,0:T(4,128)S(1)} %get-tuple-element.51) | copy-start | bytes 12292
  203.8 7.5 copy-start.55
  204.9 7.4 copy-start
  204.9 7.5 copy-start.56
  206.0 6.4 copy-start.57
  207.1 6.3 copy-start.5
  207.1 6.3 copy-start.49
  210.2 3.2 copy-start.50
  214.5 43.7 %copy-start.11 = (bf16[256,1024]{1,0:T(8,128)(2,1)S(1)}, bf16[256,1024]{1,0:T(8,128)(2,1)}, u32[]{:S(2)}) copy-start(bf16[256,1024]{1,0:T(8,128)(2,1)} %param.12) | copy-start | bytes 1572868
  217.6 352.3 %reduce-scatter.11.cloned.1.call-start = ((), (), s32[]{:S(2)}) async-start(), calls=%async_computation.11 | async-start | bytes 9437184 | tf_op jit(solution)/shard_map/reduce_scatter | solution.py:310
  271.6 4.5 copy-start.52
  271.6 332.1 %reduce-scatter.9.cloned.1.call-start = ((), (), s32[]{:S(2)}) async-start(), calls=%async_computation.10 | async-start | bytes 9437184 | tf_op jit(solution)/shard_map/reduce_scatter | solution.py:304
  320.4 9.5 %copy-start.44 = (f32[256]{0:T(256)S(1)}, f32[256]{0:T(256)}, u32[]{:S(2)}) copy-start(f32[256]{0:T(256)} %copy-done.43) | copy-start | bytes 3076
  320.4 9.5 %copy-start.47 = (f32[256]{0:T(256)S(1)}, f32[256]{0:T(256)}, u32[]{:S(2)}) copy-start(f32[256]{0:T(256)} %copy-done.46) | copy-start | bytes 3076
  335.8 349.1 %reduce-scatter.5.cloned.1.call-start = ((), (), s32[]{:S(2)}) async-start(), calls=%async_computation.8 | async-start | bytes 7077888 | tf_op jit(solution)/shard_map/reduce_scatter | solution.py:298
  335.8 4.1 copy-start.1
  336.7 4.1 copy-start.39
  351.8 3.8 copy-start.9
  351.8 3.9 copy-start.38
  361.0 3.7 copy-start.12
  365.6 3.7 copy-start.14
  380.3 3.5 copy-start.10
  385.5 168.7 %collective-permute-start.2 = (f32[2,2,256,1024]{2,3,1,0:T(8,128)S(1)}, f32[2,2,256,1024]{2,3,1,0:T(8,128)S(1)}, u32[]{:S(2)}, u32[]{:S(2)}) collective-permute-start(f32[2,2,256,1024]{2,3,1,0:T(8,128)S(1)} %slice_select_fusion), channel_id=1, source_target_pairs={{0,2},{1,3},{2,0},{3,1},{4,6},{5,7},{6,4},{7,5},{8,10},{9,11},{10,... | collective-permute-start | bytes 12582920 | tf_op jit(solution)/shard_map/ppermute | solution.py:14
  555.4 6.2 collective-permute-start.3
  567.3 207.6 %all-reduce.13.cloned.1.call-start = ((), (), s32[]{:S(2)}) async-start(), calls=%async_computation.12 | async-start | bytes 6291456 | tf_op jit(solution)/shard_map/psum | solution.py:320
  685.0 7.6 copy-start.21
  685.0 7.6 copy-start.29
  685.0 7.6 copy-start.42
  700.2 5.2 copy-start.33
  700.2 6.6 copy-start.58
  774.9 7.1 copy-start.34
  (29 other events, 51.8 us)
Sparse Core Ops, SparseCore 0:
  11.0 71.0 all-gather.5
  85.1 98.0 all-gather.9
  186.2 54.3 all-gather.7
  243.4 76.9 all-gather.11
  322.6 28.7 reduce-scatter.6
  353.5 124.7 reduce-scatter.10
  480.6 123.0 reduce-scatter.8
  606.0 78.8 reduce-scatter.4
  688.3 86.5 all-reduce.12
where the time goes:
time: 800 us; the launch traced here: 791 us
  waiting for transfers between devices  463 us (58%)
  blocking collectives  111 us (14%)
  matrix products  92.7 us (12%)
  local copies, waits for them, and re-layouts  60.8 us (8%)
  other arithmetic  43.1 us (5%)
  between operations  18 us (2%)
    ppermute x4, waiting for transfers between devices, swapped(): lax.ppermute(array, axis, [(i, i ^ 1 << distance) for i in range(lax.axis...  248 us
    reduce_scatter x1, waiting for transfers between devices, local(): lax.psum_scatter(gradients[2].astype(jnp.bfloat16), 'dev', scatter_dimens...  81.2 us
    unnamed x2, blocking collectives  62.5 us
    all_gather x1, blocking collectives, local(): lax.all_gather(b_fc1, ('grp', 'dev'), axis=0, tiled=True)  40 us
    all_gather x1, waiting for transfers between devices, local(): lax.all_gather(w_fc2, ('grp', 'dev'), axis=0, tiled=True)  38.2 us
    psum x1, waiting for transfers between devices, local(): lax.psum(shares[2].astype(jnp.bfloat16), 'grp').astype(jnp.float32)  35.7 us
    reduce_scatter x1, waiting for transfers between devices, local(): lax.psum_scatter(gradients[4].astype(jnp.bfloat16), 'dev', scatter_dimens...  33.8 us
    unnamed x140, local copies, waits for them, and re-layouts  27.2 us
  transfers between devices with their start and end apart: 13, of which 8 were waited for; matrix products, arithmetic and copies ran while one was open for 21% of the time, Pallas kernels for 0%

commit v1 on v0

v1 whole, which is shorter than its diff:
```python
import functools
import math

import jax
import jax.numpy as jnp
import numpy as np
from jax import lax
from jax.experimental import pallas as pl
from jax.experimental.pallas import tpu as pltpu
from jax.sharding import PartitionSpec as P

HEADS = 16
HD = 64
ROT = 32
MESH = pl.DeviceIdType.MESH
BF = jnp.bfloat16
F32 = jnp.float32


class Dims:
    def __init__(self, mesh, rows, width, ff):
        self.n_grp, self.n_dev = mesh.shape["grp"], mesh.shape["dev"]
        self.n_gy, self.n_zp = self.n_grp // 2, self.n_dev // 4
        assert self.n_gy == self.n_zp
        self.n_all = self.n_grp * self.n_dev
        self.rows, self.width, self.ff = rows, width, ff
        self.r1 = width // self.n_all
        self.r2 = ff // self.n_all
        self.ffs = ff // 8
        self.qs = 3 * width // 8
        self.ca = self.ffs + self.qs
        self.rd = width // self.n_dev
        self.rdg = self.rd // self.n_gy
        self.c2 = width // self.n_gy
        self.ng = self.n_gy * self.n_zp


class Me:
    def __init__(self, d):
        grp, dev = lax.axis_index("grp"), lax.axis_index("dev")
        self.grp, self.dev = grp, dev
        self.gy, self.gx = grp // 2, lax.rem(grp, 2)
        self.zp, self.q = dev // 4, lax.rem(dev, 4)
        self.zl, self.c = self.q // 2, lax.rem(self.q, 2)
        self.f = grp * d.n_dev + dev
        self.rank = self.gx * 4 + self.q


def place(gy, gx, zp, q):
    return {"grp": gy * 2 + gx, "dev": zp * 4 + q}


def remote(src, dst, send, recv, device):
    return pltpu.make_async_remote_copy(
        src_ref=src,
        dst_ref=dst,
        send_sem=send,
        recv_sem=recv,
        device_id=device,
        device_id_type=MESH,
    )


def gather_kernel(d, tok, cot, p1, wo, wf2, sm, TOK, COT, WA, WO, WF2, SM, loc, ts, tr, cs, cr,
                  w1s, w1r, m1s, m1r, zs, zr, ys, yr, os_, or_):
    me = Me(d)
    gy, gx, zp, q = me.gy, me.gx, me.zp, me.q
    half = d.rows // 2
    local = [
        pltpu.make_async_copy(tok, TOK.at[gx, q], loc.at[0]),
        pltpu.make_async_copy(cot, COT.at[gx, q], loc.at[1]),
        pltpu.make_async_copy(p1.at[me.rank], WA.at[gy, gx, zp, q], loc.at[2]),
        pltpu.make_async_copy(wf2, WF2.at[gy, zp], loc.at[3]),
        pltpu.make_async_copy(sm, SM.at[gy, gx, zp, q], loc.at[4]),
    ]

    def token_send(src, buf, send, recv, slot, bx, bq, h, device):
        return remote(
            src.at[pl.ds(h * half, half)],
            buf.at[bx, bq, pl.ds(h * half, half)],
            send.at[slot, h],
            recv.at[bx * 4 + bq, h],
            device,
        )

    x_dev, z_dev, c_dev = place(gy, 1 - gx, zp, q), place(gy, gx, zp, lax.rem(q + 2, 4)), place(
        gy, gx, zp, me.zl * 2 + 1 - me.c
    )
    qz = lax.rem(q + 2, 4)

    sends = []

    def go(copy):
        copy.start()
        sends.append(copy)

    def arrived(buf, send, recv, bx, bq, h):
        token_send(buf.at[bx, bq], buf, send, recv, 0, bx, bq, h, x_dev).wait_recv()

    for h in range(2):
        go(token_send(tok, TOK, ts, tr, 0, gx, q, h, x_dev))
        go(token_send(cot, COT, cs, cr, 0, gx, q, h, z_dev))
    for i in range(1, 8):
        other = lax.rem(me.rank + i, 8)
        dev = place(gy, other // 4, zp, lax.rem(other, 4))
        go(remote(p1.at[other], WA.at[gy, gx, zp, q], w1s.at[other], w1r.at[me.rank], dev))
        go(remote(sm, SM.at[gy, gx, zp, q], m1s.at[other], m1r.at[me.rank], dev))
    for copy in local:
        copy.start()
    for i in range(1, d.n_zp):
        oz = lax.rem(zp + i, d.n_zp)
        go(remote(wf2, WF2.at[gy, zp], zs.at[2, oz], zr.at[2, zp], place(gy, gx, oz, q)))
    per = 128 // d.r1
    owner = me.f // per
    part = lax.rem(me.f, per)
    ox, oq = owner // 4, lax.rem(owner, 4)
    for i in range(d.ng):
        group = lax.rem(gy * d.n_zp + zp + i, d.ng)
        oy, oz = group // d.n_zp, lax.rem(group, d.n_zp)
        copy = remote(wo, WO.at[part], os_.at[i], or_.at[part], place(oy, ox, oz, oq))
        if i == 0:
            mine = jnp.logical_and(ox == gx, oq == q)

            @pl.when(mine)
            def _():
                here = pltpu.make_async_copy(wo, WO.at[part], loc.at[5])
                here.start()
                here.wait()

            @pl.when(jnp.logical_not(mine))
            def _():
                copy.start()
                copy.wait_send()
        else:
            go(copy)
    for h in range(2):
        go(token_send(tok, TOK, ts, tr, 1, gx, q, h, z_dev))
        go(token_send(cot, COT, cs, cr, 1, gx, q, h, x_dev))
        go(token_send(tok, TOK, ts, tr, 3, gx, q, h, c_dev))
        go(token_send(cot, COT, cs, cr, 3, gx, q, h, c_dev))
    for h in range(2):
        arrived(TOK, ts, tr, 1 - gx, q, h)
        go(token_send(TOK.at[1 - gx, q], TOK, ts, tr, 2, 1 - gx, q, h, z_dev))
        go(token_send(TOK.at[1 - gx, q], TOK, ts, tr, 4, 1 - gx, q, h, c_dev))
        arrived(COT, cs, cr, gx, qz, h)
        go(token_send(COT.at[gx, qz], COT, cs, cr, 2, gx, qz, h, x_dev))
        go(token_send(COT.at[gx, qz], COT, cs, cr, 4, gx, qz, h, c_dev))
    for copy in local:
        copy.wait()
    for i in range(1, 8):
        other = lax.rem(me.rank + i, 8)
        ox_, oq_ = other // 4, lax.rem(other, 4)
        dev = place(gy, ox_, zp, oq_)
        remote(p1.at[0], WA.at[gy, ox_, zp, oq_], w1s.at[other], w1r.at[other], dev).wait_recv()
        remote(sm, SM.at[gy, ox_, zp, oq_], m1s.at[other], m1r.at[other], dev).wait_recv()
    for i in range(1, d.n_zp):
        oz = lax.rem(zp + i, d.n_zp)
        dev = place(gy, gx, oz, q)
        go(remote(WA.at[gy, :, zp], WA.at[gy, :, zp], zs.at[0, oz], zr.at[0, zp], dev))
        go(remote(SM.at[gy, :, zp], SM.at[gy, :, zp], zs.at[1, oz], zr.at[1, zp], dev))
    for i in range(1, d.n_zp):
        oz = lax.rem(zp + i, d.n_zp)
        remote(wf2, WF2.at[gy, oz], zs.at[2, oz], zr.at[2, oz], place(gy, gx, oz, q)).wait_recv()
    for i in range(1, d.n_gy):
        oy = lax.rem(gy + i, d.n_gy)
        go(remote(WF2.at[gy], WF2.at[gy], ys.at[2, oy], yr.at[2, gy], place(oy, gx, zp, q)))
    for h in range(2):
        arrived(TOK, ts, tr, gx, qz, h)
        go(token_send(TOK.at[gx, qz], TOK, ts, tr, 5, gx, qz, h, c_dev))
        arrived(COT, cs, cr, 1 - gx, q, h)
        go(token_send(COT.at[1 - gx, q], COT, cs, cr, 5, 1 - gx, q, h, c_dev))
    for h in range(2):
        arrived(TOK, ts, tr, 1 - gx, qz, h)
        go(token_send(TOK.at[1 - gx, qz], TOK, ts, tr, 6, 1 - gx, qz, h, c_dev))
        arrived(COT, cs, cr, 1 - gx, qz, h)
        go(token_send(COT.at[1 - gx, qz], COT, cs, cr, 6, 1 - gx, qz, h, c_dev))
    for i in range(1, d.n_zp):
        oz = lax.rem(zp + i, d.n_zp)
        dev = place(gy, gx, oz, q)
        remote(WA.at[gy, :, oz], WA.at[gy, :, oz], zs.at[0, oz], zr.at[0, oz], dev).wait_recv()
        remote(SM.at[gy, :, oz], SM.at[gy, :, oz], zs.at[1, oz], zr.at[1, oz], dev).wait_recv()
    for i in range(1, d.n_gy):
        oy = lax.rem(gy + i, d.n_gy)
        dev = place(oy, gx, zp, q)
        go(remote(WA.at[gy], WA.at[gy], ys.at[0, oy], yr.at[0, gy], dev))
        go(remote(SM.at[gy], SM.at[gy], ys.at[1, oy], yr.at[1, gy], dev))
    qc = me.zl * 2 + 1 - me.c
    qcz = lax.rem(qc + 2, 4)
    for bx in (gx, 1 - gx):
        for bq in (qc, qcz):
            for h in range(2):
                arrived(TOK, ts, tr, bx, bq, h)
                arrived(COT, cs, cr, bx, bq, h)
    for i in range(1, d.n_gy):
        oy = lax.rem(gy + i, d.n_gy)
        dev = place(oy, gx, zp, q)
        for k, buf in enumerate((WA, SM, WF2)):
            remote(buf.at[oy], buf.at[oy], ys.at[k, oy], yr.at[k, oy], dev).wait_recv()
    for i in range(per):
        source = me.rank * per + i

        @pl.when(source != me.f)
        def _():
            remote(wo, WO.at[i], os_.at[0], or_.at[i], x_dev).wait_recv()

    for copy in sends:
        copy.wait_send()


def gather(d, tok, cot, p1, wo, wf2, sm):
    any_spec = pl.BlockSpec(memory_space=pl.ANY)
    dma = pltpu.SemaphoreType.DMA
    shape = jax.ShapeDtypeStruct
    return pl.pallas_call(
        functools.partial(gather_kernel, d),
        out_shape=(
            shape((2, 4, d.rows, d.width), BF),
            shape((2, 4, d.rows, d.width), BF),
            shape((d.n_gy, 2, d.n_zp, 4, d.r1, d.ca), BF),
            shape((128 // d.r1, d.r1, d.width), BF),
            shape((d.n_gy, d.n_zp, d.r2, d.width), BF),
            shape((d.n_gy, 2, d.n_zp, 4, 16, 128), BF),
        ),
        in_specs=[any_spec] * 6,
        out_specs=(any_spec,) * 6,
        scratch_shapes=[
            dma((6,)), dma((7, 2)), dma((8, 2)), dma((7, 2)), dma((8, 2)),
            dma((8,)), dma((8,)), dma((8,)), dma((8,)),
            dma((3, d.n_zp)), dma((3, d.n_zp)), dma((3, d.n_gy)), dma((3, d.n_gy)),
            dma((d.ng,)), dma((128 // d.r1,)),
        ],
        compiler_params=pltpu.CompilerParams(has_side_effects=True),
        name="gather",
    )(tok, cot, p1, wo, wf2, sm)


def add_blocks(out, *terms):
    n = out.shape[0]

    @pl.loop(0, n)
    def _(i):
        total = terms[0][i].astype(F32)
        for term in terms[1:]:
            total = total + term[i].astype(F32)
        out[i] = total.astype(out.dtype)


def reduce_kernel(d, mix, gh, ga, gf2, gwo, smg, MIX, GH, FA, FF2, FWO, FSM,
                  mt, m2, m3, ht, h2, h3, ya, y2, yo, za, z2, zo, s1, s2,
                  tsem, asem, fsem, osem, ssem, dsem):
    me = Me(d)
    gy, gx, zp, q, zl, c = me.gy, me.gx, me.zp, me.q, me.zl, me.c
    x_dev, z_dev, c_dev = place(gy, 1 - gx, zp, q), place(gy, gx, zp, lax.rem(q + 2, 4)), place(
        gy, gx, zp, zl * 2 + 1 - c
    )
    sends = []

    def go(copy):
        copy.start()
        sends.append(copy)

    for i in range(1, d.n_gy):
        oy = lax.rem(gy + i, d.n_gy)
        dev = place(oy, gx, zp, q)
        go(remote(gf2.at[:, :, oy], y2.at[gy], fsem.at[0, 0, oy], fsem.at[0, 1, gy], dev))
        go(remote(gwo.at[oy], yo.at[gy], osem.at[0, 0, oy], osem.at[0, 1, gy], dev))
        go(remote(ga.at[:, :, oy], ya.at[gy], asem.at[0, 0, oy], asem.at[0, 1, gy], dev))
    row_sums = ((mix, mt, m2, m3, MIX, 0), (gh, ht, h2, h3, GH, 1))
    for src, t_buf, _, _, _, k in row_sums:
        go(remote(src.at[:, :, 1 - c], t_buf, tsem.at[k, 0, 0], tsem.at[k, 1, 0], c_dev))
    for i in range(1, 8):
        other = lax.rem(me.rank + i, 8)
        oq = lax.rem(other, 4)
        go(remote(smg.at[oq], s1.at[me.rank], ssem.at[0, 0, other], ssem.at[0, 1, me.rank],
                  place(gy, other // 4, zp, oq)))
    for src, t_buf, b2, b3, _, k in row_sums:
        remote(src.at[:, :, 1 - c], t_buf, tsem.at[k, 0, 0], tsem.at[k, 1, 0], c_dev).wait_recv()
        for bx in range(2):
            for bz in range(2):
                add_blocks(t_buf.at[bx, bz], t_buf.at[bx, bz], src.at[bx, bz, c])
        if k == 0:
            go(remote(t_buf.at[1 - gx], b2, tsem.at[k, 0, 1], tsem.at[k, 1, 1], x_dev))
        else:
            go(remote(t_buf.at[:, 1 - zl], b2, tsem.at[k, 0, 1], tsem.at[k, 1, 1], z_dev))
    for i in range(1, d.n_gy):
        oy = lax.rem(gy + i, d.n_gy)
        dev = place(oy, gx, zp, q)
        remote(gf2.at[:, :, oy], y2.at[oy], fsem.at[0, 0, oy], fsem.at[0, 1, oy], dev).wait_recv()
        remote(gwo.at[oy], yo.at[oy], osem.at[0, 0, oy], osem.at[0, 1, oy], dev).wait_recv()
    others = [lax.rem(gy + i, d.n_gy) for i in range(1, d.n_gy)]
    for a in range(d.n_gy):
        for b in range(d.n_zp):
            add_blocks(y2.at[gy, a, b], gf2.at[a, b, gy], *[y2.at[o, a, b] for o in others])
    add_blocks(yo.at[gy], gwo.at[gy], *[yo.at[o] for o in others])
    for i in range(1, d.n_zp):
        oz = lax.rem(zp + i, d.n_zp)
        dev = place(gy, gx, oz, q)
        go(remote(y2.at[gy, oz], z2.at[zp], fsem.at[1, 0, oz], fsem.at[1, 1, zp], dev))
        go(remote(yo.at[gy], zo.at[zp], osem.at[1, 0, oz], osem.at[1, 1, zp], dev))
    for i in range(1, d.n_gy):
        oy = lax.rem(gy + i, d.n_gy)
        dev = place(oy, gx, zp, q)
        remote(ga.at[:, :, oy], ya.at[oy], asem.at[0, 0, oy], asem.at[0, 1, oy], dev).wait_recv()
    for a in range(d.n_zp):
        for b in range(4):
            add_blocks(ya.at[gy, a, b], ga.at[a, b, gy], *[ya.at[o, a, b] for o in others])
    for i in range(1, d.n_zp):
        oz = lax.rem(zp + i, d.n_zp)
        go(remote(ya.at[gy, oz], za.at[zp], asem.at[1, 0, oz], asem.at[1, 1, zp],
                  place(gy, gx, oz, q)))
    for i in range(1, 8):
        other = lax.rem(me.rank + i, 8)
        remote(smg.at[0], s1.at[other], ssem.at[0, 0, other], ssem.at[0, 1, other],
               x_dev).wait_recv()
    s1[me.rank] = smg[q]
    total = s1[0]
    for i in range(1, 8):
        total = total + s1[i]
    s2[d.ng] = total
    own_group = gy * d.n_zp + zp
    for i in range(1, d.ng):
        group = lax.rem(own_group + i, d.ng)
        oy, oz = group // d.n_zp, lax.rem(group, d.n_zp)
        go(remote(s2.at[d.ng, oz], s2.at[own_group, 0], ssem.at[1, 0, group],
                  ssem.at[1, 1, own_group], place(oy, gx, oz, q)))
    for src, t_buf, b2, b3, _, k in row_sums:
        if k == 0:
            remote(t_buf.at[1 - gx], b2, tsem.at[k, 0, 1], tsem.at[k, 1, 1], x_dev).wait_recv()
            for b in range(2):
                add_blocks(b2.at[b], b2.at[b], t_buf.at[gx, b])
            go(remote(b2.at[1 - zl], b3, tsem.at[k, 0, 2], tsem.at[k, 1, 2], z_dev))
        else:
            remote(t_buf.at[:, 1 - zl], b2, tsem.at[k, 0, 1], tsem.at[k, 1, 1], z_dev).wait_recv()
            for b in range(2):
                add_blocks(b2.at[b], b2.at[b], t_buf.at[b, zl])
            go(remote(b2.at[1 - gx], b3, tsem.at[k, 0, 2], tsem.at[k, 1, 2], x_dev))
    zothers = [lax.rem(zp + i, d.n_zp) for i in range(1, d.n_zp)]
    for o in zothers:
        dev = place(gy, gx, o, q)
        remote(y2.at[gy, o], z2.at[o], fsem.at[1, 0, o], fsem.at[1, 1, o], dev).wait_recv()
        remote(yo.at[gy], zo.at[o], osem.at[1, 0, o], osem.at[1, 1, o], dev).wait_recv()
    hz = d.n_zp // 2
    for b in range(d.n_zp):
        add_blocks(z2.at[zp, b], y2.at[gy, zp, b], *[z2.at[o, b] for o in zothers])
    add_blocks(zo.at[zp], yo.at[gy], *[zo.at[o] for o in zothers])
    for j in range(2):
        dq = gx * 2 + j
        for ox in range(2):
            mine = jnp.logical_and(ox == gx, dq == q)
            src = z2.at[zp, pl.ds(j * hz, hz)]
            dst = FF2.at[gy, q]
            copy = remote(src, dst, dsem.at[0, 0, j * 2 + ox], dsem.at[0, 1, q],
                          place(gy, ox, zp, dq))

            @pl.when(mine)
            def _():
                here = pltpu.make_async_copy(src, dst, dsem.at[0, 2, 0])
                here.start()
                here.wait()

            @pl.when(jnp.logical_not(mine))
            def _():
                copy.start()
    nwo = 128 // d.rd
    wo_zp = me.rank * d.n_zp // 8
    for j in range(nwo):
        dq = lax.rem(me.rank * nwo + j, 4)
        for ox in range(2):
            here_too = jnp.logical_and(ox == gx, dq == q)
            src = zo.at[zp, pl.ds(j * (d.rd // 16), d.rd // 16)]
            dst = FWO.at[gy]
            copy = remote(src, dst, dsem.at[1, 0, j * 2 + ox], dsem.at[1, 1, 0],
                          place(gy, ox, zp, dq))

            @pl.when(jnp.logical_and(wo_zp == zp, here_too))
            def _():
                here = pltpu.make_async_copy(src, dst, dsem.at[1, 2, 0])
                here.start()
                here.wait()

            @pl.when(jnp.logical_and(wo_zp == zp, jnp.logical_not(here_too)))
            def _():
                copy.start()
    for o in zothers:
        dev = place(gy, gx, o, q)
        remote(ya.at[gy, o], za.at[o], asem.at[1, 0, o], asem.at[1, 1, o], dev).wait_recv()
    for b in range(4):
        add_blocks(za.at[zp, b], ya.at[gy, zp, b], *[za.at[o, b] for o in zothers])
    for i in range(1, 8):
        other = lax.rem(me.rank + i, 8)
        ox, oq = other // 4, lax.rem(other, 4)
        go(remote(za.at[zp, oq], FA.at[gy, gx, q], dsem.at[2, 0, other],
                  dsem.at[2, 1, me.rank], place(gy, ox, zp, oq)))
    here = pltpu.make_async_copy(za.at[zp, q], FA.at[gy, gx, q], dsem.at[2, 2, 0])
    here.start()
    here.wait()
    for src, t_buf, b2, b3, out, k in row_sums:
        if k == 0:
            remote(b2.at[1 - zl], b3, tsem.at[k, 0, 2], tsem.at[k, 1, 2], z_dev).wait_recv()
            mine = b2.at[zl]
        else:
            remote(b2.at[1 - gx], b3, tsem.at[k, 0, 2], tsem.at[k, 1, 2], x_dev).wait_recv()
            mine = b2.at[gx]
        n = out.shape[0]
        for i in range(n):
            out[i] = mine[i].astype(F32) + b3[i].astype(F32)
    for sq in range(4):
        away = jnp.logical_not(jnp.logical_and(gx == zl, sq == q))

        @pl.when(away)
        def _():
            remote(z2.at[0, pl.ds(0, hz)], FF2.at[gy, sq], dsem.at[0, 0, 0], dsem.at[0, 1, sq],
                   x_dev).wait_recv()
    source = (zp * 4 + q) // nwo
    sx, sq = source // 4, lax.rem(source, 4)

    @pl.when(jnp.logical_not(jnp.logical_and(sx == gx, sq == q)))
    def _():
        remote(zo.at[0, pl.ds(0, d.rd // 16)], FWO.at[gy], dsem.at[1, 0, 0], dsem.at[1, 1, 0],
               x_dev).wait_recv()
    for o in others:
        dev = place(o, gx, zp, q)
        go(remote(FF2.at[gy], FF2.at[gy], fsem.at[2, 0, o], fsem.at[2, 1, gy], dev))
        go(remote(FWO.at[gy], FWO.at[gy], osem.at[2, 0, o], osem.at[2, 1, gy], dev))
    for i in range(1, 8):
        other = lax.rem(me.rank + i, 8)
        ox, oq = other // 4, lax.rem(other, 4)
        remote(za.at[0, 0], FA.at[gy, ox, oq], dsem.at[2, 0, other], dsem.at[2, 1, other],
               x_dev).wait_recv()
    for o in others:
        dev = place(o, gx, zp, q)
        go(remote(FA.at[gy], FA.at[gy], asem.at[2, 0, o], asem.at[2, 1, gy], dev))
    for i in range(1, d.ng):
        group = lax.rem(own_group + i, d.ng)
        remote(s2.at[d.ng, 0], s2.at[group, 0], ssem.at[1, 0, group], ssem.at[1, 1, group],
               x_dev).wait_recv()
    total = s2[d.ng, zp]
    for i in range(1, d.ng):
        total = total + s2[lax.rem(own_group + i, d.ng), 0]
    FSM[...] = total
    for o in others:
        dev = place(o, gx, zp, q)
        for buf, sem in ((FF2, fsem), (FWO, osem), (FA, asem)):
            remote(buf.at[o], buf.at[o], sem.at[2, 0, o], sem.at[2, 1, o], dev).wait_recv()
    for copy in sends:
        copy.wait_send()
    for j in range(2):
        for ox in range(2):
            away = jnp.logical_not(jnp.logical_and(ox == gx, gx * 2 + j == q))

            @pl.when(away)
            def _():
                remote(z2.at[zp, pl.ds(j * hz, hz)], FF2.at[gy, q], dsem.at[0, 0, j * 2 + ox],
                       dsem.at[0, 1, q], x_dev).wait_send()
    for j in range(nwo):
        dq = lax.rem(me.rank * nwo + j, 4)
        for ox in range(2):
            away = jnp.logical_not(jnp.logical_and(ox == gx, dq == q))

            @pl.when(jnp.logical_and(wo_zp == zp, away))
            def _():
                remote(zo.at[zp, pl.ds(j * (d.rd // 16), d.rd // 16)], FWO.at[gy], dsem.at[1, 0, j * 2 + ox],
                       dsem.at[1, 1, 0], x_dev).wait_send()


def reduce_all(d, mix, gh, ga, gf2, gwo, smg):
    vm = pl.BlockSpec(memory_space=pltpu.VMEM)
    dma = pltpu.SemaphoreType.DMA
    shape = jax.ShapeDtypeStruct
    R = d.rows
    slabs = R // 16
    return pl.pallas_call(
        functools.partial(reduce_kernel, d),
        out_shape=(
            shape((slabs, 16, d.width), F32),
            shape((slabs, 16, d.width), F32),
            shape((d.n_gy, 2, 4, d.rdg // 16, 16, d.ca), BF),
            shape((d.n_gy, 4, d.n_zp // 2, d.r2 // 16, 16, d.c2), BF),
            shape((d.n_gy, d.rd // 16, 16, d.c2), BF),
            shape((8, 128), F32),
        ),
        in_specs=[vm] * 6,
        out_specs=(vm,) * 6,
        scratch_shapes=[
            pltpu.VMEM((2, 2, slabs, 16, d.width), BF),
            pltpu.VMEM((2, slabs, 16, d.width), BF),
            pltpu.VMEM((slabs, 16, d.width), BF),
            pltpu.VMEM((2, 2, slabs, 16, d.width), BF),
            pltpu.VMEM((2, slabs, 16, d.width), BF),
            pltpu.VMEM((slabs, 16, d.width), BF),
            pltpu.VMEM((d.n_gy, d.n_zp, 4, d.rdg // 16, 16, d.ca), BF),
            pltpu.VMEM((d.n_gy, d.n_gy, d.n_zp, d.r2 // 16, 16, d.c2), BF),
            pltpu.VMEM((d.n_gy, 8, 16, d.c2), BF),
            pltpu.VMEM((d.n_zp, 4, d.rdg // 16, 16, d.ca), BF),
            pltpu.VMEM((d.n_zp, d.n_zp, d.r2 // 16, 16, d.c2), BF),
            pltpu.VMEM((d.n_zp, 8, 16, d.c2), BF),
            pltpu.VMEM((8, d.n_zp, 8, 128), F32),
            pltpu.VMEM((d.ng + 1, d.n_zp, 8, 128), F32),
            dma((2, 2, 3)),
            dma((3, 2, max(d.n_gy, d.n_zp))),
            dma((3, 2, max(d.n_gy, d.n_zp))),
            dma((3, 2, max(d.n_gy, d.n_zp))),
            dma((2, 2, max(8, d.ng))),
            dma((3, 3, 8)),
        ],
        compiler_params=pltpu.CompilerParams(
            has_side_effects=True, vmem_limit_bytes=62 * 1024 * 1024
        ),
        name="reduce",
    )(mix, gh, ga, gf2, gwo, smg)


def gelu_parts(v):
    tangent = jnp.tanh(0.7978845608028654 * (v + 0.044715 * v * v * v))
    inner = 0.7978845608028654 * (1.0 + 0.134145 * v * v)
    act = 0.5 * v * (1.0 + tangent)
    slope = 0.5 * (1.0 + tangent) + 0.5 * v * (1.0 - tangent * tangent) * inner
    return act, slope


def places_of_slot(rows):
    slot = 4 * rows
    row = jnp.arange(slot, dtype=jnp.int32)
    piece, inner, half = row // rows, row % rows, rows // 2
    return jnp.where(inner < half, piece * half + inner, slot - (piece + 1) * half + inner - half)


def spread(vec, lane):
    n = vec.shape[0]
    if n == 128:
        return vec
    tiled = jnp.tile(vec, 128 // n)
    at = jnp.arange(128, dtype=jnp.int32) // n
    return jnp.where(at == lane, tiled, jnp.zeros_like(tiled))


def dot(a, b, dims):
    return lax.dot_general(a, b, (dims, ((), ())), preferred_element_type=F32)


def local(d, tokens, cotangent, lengths, offsets, ln_gain, ln_bias, w_qkv, w_out, w_fc1, b_fc1,
          w_fc2, b_fc2):
    me = Me(d)
    R, W = d.rows, d.width
    fc1 = w_fc1.reshape(d.r1, d.n_gy, 2, d.n_zp, 4, d.r2).transpose(2, 4, 0, 1, 3, 5)
    fc1 = fc1.reshape(8, d.r1, d.ffs)
    qkv = w_qkv.reshape(d.r1, 3, 8, 128).transpose(2, 0, 1, 3).reshape(8, d.r1, d.qs)
    p1 = jnp.concatenate([fc1, qkv], axis=2)
    lane = lax.rem(me.f, 128 // d.r1)
    pad = jnp.zeros((128 - d.r2,), BF)
    sm = jnp.stack([spread(ln_gain, lane), spread(ln_bias, lane), spread(b_fc2, lane),
                    jnp.concatenate([b_fc1, pad]) if d.r2 < 128 else b_fc1])
    sm = jnp.concatenate([sm, jnp.zeros((12, 128), BF)])
    TOK, COT, WA, WO, WF2, SM = gather(d, tokens, cotangent, p1, w_out, w_fc2, sm)
    sums = SM.reshape(8, d.n_all // 8, 16, 128).astype(F32).sum(axis=1)
    gain, bias, bfc2 = sums[:, 0].reshape(W), sums[:, 1].reshape(W), sums[:, 2].reshape(W)
    mine = lax.dynamic_index_in_dim(
        lax.dynamic_index_in_dim(SM, me.gx, 1, False), me.q, 2, False
    )
    bfc1 = mine[:, :, 3, : d.r2].reshape(d.ffs).astype(F32)
    WA = WA.reshape(W, d.ca)
    wfc1, wqkv = WA[:, : d.ffs], WA[:, d.ffs :]
    wout = WO.reshape(128, W)
    wfc2 = WF2.reshape(d.ffs, W)
    slot0 = (me.gy * 2) * d.n_zp + me.zp
    lens = jnp.stack([lengths[slot0], lengths[slot0 + d.n_zp]])
    offs = jnp.stack([offsets[slot0], offsets[slot0 + d.n_zp]])
    places = places_of_slot(R)
    live = (places[None] >= offs[:, None]) & (places[None] < (offs + lens)[:, None])
    live_f = live.reshape(8 * R, 1).astype(F32)
    tok = TOK.reshape(8 * R, W).astype(F32)
    centred = tok - jnp.mean(tok, axis=-1, keepdims=True)
    inverse = lax.rsqrt(jnp.mean(centred * centred, axis=-1, keepdims=True) + 1e-5)
    normed = centred * inverse
    h = (normed * gain + bias).astype(BF)
    grad_y = (COT.reshape(8 * R, W).astype(F32) * live_f).astype(BF)
    qkv = dot(h, wqkv, ((1,), (0,)))
    freq = jnp.exp(jnp.arange(ROT // 2, dtype=F32) * (-2.0 * math.log(10000.0) / ROT))
    angles = (places[None] - offs[:, None]).astype(F32).reshape(8 * R)[:, None] * freq[None]
    cos, sin = jnp.cos(angles)[:, None], jnp.sin(angles)[:, None]

    def turn(x, sign):
        a, b = x[..., : ROT // 2], x[..., ROT // 2 : ROT]
        return jnp.concatenate(
            [a * cos - sign * b * sin, b * cos + sign * a * sin, x[..., ROT:]], axis=-1
        )

    queries = turn(qkv[:, :128].reshape(8 * R, 2, HD), 1.0).astype(BF).reshape(2, 4 * R, 2, HD)
    keys = turn(qkv[:, 128:256].reshape(8 * R, 2, HD), 1.0).astype(BF).reshape(2, 4 * R, 2, HD)
    values = qkv[:, 256:].astype(BF).reshape(2, 4 * R, 2, HD)
    scores = jnp.einsum("sqhd,skhd->shqk", queries, keys, preferred_element_type=F32) * 0.125
    allowed = (places[None, None, :] <= places[None, :, None]) & (
        live[:, None, :] | (places[None, None, :] == places[None, :, None])
    )
    scores = jnp.where(allowed[:, None], scores, -1e30)
    expo = jnp.exp(scores - jnp.max(scores, axis=-1, keepdims=True))
    prob = expo / jnp.sum(expo, axis=-1, keepdims=True)
    low = prob.astype(BF)
    att = jnp.einsum("shqk,skhd->sqhd", low, values, preferred_element_type=F32)
    att = att.astype(BF).reshape(8 * R, 128)
    pre = dot(h, wfc1, ((1,), (0,))) + bfc1
    act, slope = gelu_parts(pre)
    act = act.astype(BF)
    mix = dot(att, wout, ((1,), (0,))) + dot(act, wfc2, ((1,), (0,)))
    g_wo = dot(att, grad_y, ((0,), (0,)))
    g_f2 = dot(act, grad_y, ((0,), (0,)))
    grad_pre = (dot(grad_y, wfc2, ((1,), (1,))) * slope).astype(BF)
    g_f1 = dot(h, grad_pre, ((0,), (0,)))
    g_bf1 = grad_pre.astype(F32).sum(axis=0)
    grad_att = dot(grad_y, wout, ((1,), (1,))).astype(BF).reshape(2, 4 * R, 2, HD)
    g_prob = jnp.einsum("sqhd,skhd->shqk", grad_att, values, preferred_element_type=F32)
    row_dot = jnp.sum(prob * g_prob, axis=-1, keepdims=True)
    g_score = (prob * (g_prob - row_dot)).astype(BF)
    g_v = jnp.einsum("shqk,sqhd->skhd", low, grad_att, preferred_element_type=F32)
    g_q = jnp.einsum("shqk,skhd->sqhd", g_score, keys, preferred_element_type=F32) * 0.125
    g_k = jnp.einsum("shqk,sqhd->skhd", g_score, queries, preferred_element_type=F32) * 0.125
    g_q = turn(g_q.reshape(8 * R, 2, HD), -1.0).reshape(8 * R, 128)
    g_k = turn(g_k.reshape(8 * R, 2, HD), -1.0).reshape(8 * R, 128)
    g_qkv = jnp.concatenate([g_q, g_k, g_v.reshape(8 * R, 128)], axis=1).astype(BF)
    g_wqkv = dot(h, g_qkv, ((0,), (0,)))
    gh = dot(grad_pre, wfc1, ((1,), (1,))) + dot(g_qkv, wqkv, ((1,), (1,)))
    g_gain, g_bias = (gh * normed).sum(axis=0), gh.sum(axis=0)
    g_bf2 = jnp.where(me.rank == 0, grad_y.astype(F32).sum(axis=0), 0.0)
    nd, per = d.n_dev, W // d.n_dev

    def wide(x):
        x = x.reshape(nd, -1)
        n = x.shape[1]
        if n < 128:
            x = jnp.concatenate([x, jnp.zeros((nd, 128 - n), F32)], axis=1)
        return x.reshape(nd, -1, 128)

    bf1_rows = max(d.ff // nd // 128, 1)
    full = jnp.zeros((d.n_gy, 2, d.n_zp, 4, d.r2), F32)
    full = lax.dynamic_update_slice(
        full, g_bf1.reshape(d.n_gy, 1, d.n_zp, 1, d.r2), (0, me.gx, 0, me.q, 0)
    )
    smg = jnp.concatenate(
        [wide(g_gain), wide(g_bias), wide(g_bf2), wide(full.reshape(d.ff)),
         jnp.zeros((nd, 5 - bf1_rows, 128), F32)], axis=1,
    )
    smg = smg.reshape(d.n_zp, 4, 8, 128).transpose(1, 0, 2, 3)
    slabs = R // 16
    mix_p = mix.astype(BF).reshape(2, 2, 2, slabs, 16, W)
    gh_p = gh.astype(BF).reshape(2, 2, 2, slabs, 16, W)
    ga = jnp.concatenate([g_f1, g_wqkv], axis=1).astype(BF)
    ga = ga.reshape(d.n_zp, 4, d.n_gy, d.rdg // 16, 16, d.ca)
    gf2 = g_f2.astype(BF).reshape(d.n_gy, d.n_zp, d.r2 // 16, 16, d.n_gy, d.c2)
    gf2 = gf2.transpose(0, 1, 4, 2, 3, 5)
    gwo = g_wo.astype(BF).reshape(8, 16, d.n_gy, d.c2).transpose(2, 0, 1, 3)
    MIX, GH, FA, FF2, FWO, FSM = reduce_all(d, mix_p, gh_p, ga, gf2, gwo, smg)
    own = me.gx * 4 + me.q

    def own_rows(x):
        return lax.dynamic_index_in_dim(x.reshape(8, R, x.shape[-1]), own, 0, False)

    my_live, my_normed, my_inv = own_rows(live_f), own_rows(normed), own_rows(inverse)
    mixed = (my_live * (tokens.astype(F32) + MIX.reshape(R, W) + bfc2)).astype(BF)
    scaled = GH.reshape(R, W) * gain
    grad_norm = my_inv * (
        scaled - jnp.mean(scaled, axis=-1, keepdims=True)
        - my_normed * jnp.mean(scaled * my_normed, axis=-1, keepdims=True)
    )
    token_grad = (cotangent.astype(F32) * my_live + grad_norm).astype(BF)
    FA = FA.reshape(d.n_gy, 2, 4, d.rdg, d.ca)
    o_f1 = FA[..., : d.ffs].reshape(d.n_gy, 2, 4, d.rdg, d.n_gy, d.n_zp, d.r2)
    o_f1 = o_f1.transpose(0, 3, 4, 1, 5, 2, 6).reshape(d.rd, d.ff).astype(F32)
    o_qkv = FA[..., d.ffs :].reshape(d.n_gy, 8, d.rdg, 3, 128)
    o_qkv = o_qkv.transpose(0, 2, 3, 1, 4).reshape(d.rd, 3 * W).astype(F32)
    o_f2 = FF2.reshape(d.n_gy, 4, d.n_zp // 2, d.r2, d.c2).transpose(2, 1, 3, 0, 4)
    o_f2 = o_f2.reshape(d.ff // nd, W).astype(F32)
    o_wo = FWO.reshape(d.n_gy, d.rd, d.c2).transpose(1, 0, 2).reshape(d.rd, W).astype(F32)
    o_gain, o_bias, o_bf2 = FSM[0, :per], FSM[1, :per], FSM[2, :per]
    o_bf1 = FSM[3 : 3 + bf1_rows].reshape(-1)[: d.ff // nd]
    return mixed, token_grad, o_gain, o_bias, o_qkv, o_wo, o_f1, o_bf1, o_f2, o_bf2


def cdot(a, b, ca, cb):
    return lax.dot_general(a, b, (((ca,), (cb,)), ((), ())), preferred_element_type=F32)


def rows_at(start, n):
    return pl.ds(pl.multiple_of(start, n), n)


def layer_kernel(d, lens, offs, tok, cot, wqkv, wo, wfc1, wf2, sm, c0, s0,
                 MIXED, TGRAD, F1, FQ, F2, FWO, FSM,
                 TOK, COT, H, HT, Q, K, V, KT, VT, P0, P1, P2, P3, ACT, AT, SG, ATT, GATT, GQKV,
                 DK, DV, MIXP, WF1, WQ, WF2, WO, SM, VEC, BF1, SMG, SUMS, OWN,
                 mt, m2, m3, ht, h2, h3, GB, GA, GQ, yb, ya, yq, zb, za, zq, s1, s2,
                 loc, ts, tr, cs, cr, w1s, w1r, zs, zr, ys, yr, os_, or_,
                 tsem, bsem, asem, qsem, ssem, dsem):
    me = Me(d)
    gy, gx, zp, q, zl, c = me.gy, me.gx, me.zp, me.q, me.zl, me.c
    half, R, W = d.rows // 2, d.rows, d.width
    S = 4 * R
    PT = (P0, P1, P2, P3)
    qz, qc = lax.rem(q + 2, 4), zl * 2 + 1 - c
    qcz = lax.rem(qc + 2, 4)
    x_dev, z_dev, c_dev = place(gy, 1 - gx, zp, q), place(gy, gx, zp, qz), place(gy, gx, zp, qc)
    oz, oy = 1 - zp, 1 - gy
    zz_dev, yy_dev = place(gy, gx, oz, q), place(oy, gx, zp, q)
    sends, cot_sends = [], []

    def go(copy, kept=sends):
        copy.start()
        kept.append(copy)

    def block(bx, bq, h):
        pb = bq if h == 0 else 7 - bq
        return rows_at(bx * S + pb * half, half)

    def tsend(src, buf, send, recv, slot, bx, bq, h, device):
        return remote(src, buf.at[block(bx, bq, h)], send.at[slot, h], recv.at[bx * 4 + bq, h], device)

    TOKS, COTS = (tok, TOK, ts, tr, sends), (cot, COT, cs, cr, cot_sends)

    def x_first(arr, h):
        return arr is TOKS and h == 0

    def own_half(src, h):
        return src.at[pl.ds(h * half, half)]

    def first(arr, h):
        src, buf, send, recv, kept = arr
        go(tsend(own_half(src, h), buf, send, recv, 0, gx, q, h, x_dev if x_first(arr, h) else z_dev), kept)

    def second(arr, h):
        src, buf, send, recv, kept = arr
        go(tsend(own_half(src, h), buf, send, recv, 1, gx, q, h, z_dev if x_first(arr, h) else x_dev), kept)
        go(tsend(own_half(src, h), buf, send, recv, 3, gx, q, h, c_dev), kept)

    def wait_block(arr, bx, bq, h):
        _, buf, send, recv, kept = arr
        tsend(buf.at[block(bx, bq, h)], buf, send, recv, 0, bx, bq, h, x_dev).wait_recv()

    def pass_on(arr, slot, bx, bq, h, device):
        _, buf, send, recv, kept = arr
        go(tsend(buf.at[block(bx, bq, h)], buf, send, recv, slot, bx, bq, h, device), kept)

    def relay_first(arr, h):
        bx, bq = (1 - gx, q) if x_first(arr, h) else (gx, qz)
        wait_block(arr, bx, bq, h)
        pass_on(arr, 2, bx, bq, h, z_dev if x_first(arr, h) else x_dev)
        pass_on(arr, 4, bx, bq, h, c_dev)

    def relay_second(arr, h):
        bx, bq = (gx, qz) if x_first(arr, h) else (1 - gx, q)
        wait_block(arr, bx, bq, h)
        pass_on(arr, 5, bx, bq, h, c_dev)
        wait_block(arr, 1 - gx, qz, h)
        pass_on(arr, 6, 1 - gx, qz, h, c_dev)

    def wait_twin(arr):
        for bx in (gx, 1 - gx):
            for bq in (qc, qcz):
                for h in range(2):
                    wait_block(arr, bx, bq, h)

    own_rows = rows_at(q * d.r1, d.r1)
    local = [
        pltpu.make_async_copy(sm, SM.at[gy, gx, zp, q], loc.at[0]),
        pltpu.make_async_copy(wf2, WF2.at[gy, zp], loc.at[1]),
    ]
    for h in range(2):
        local.append(pltpu.make_async_copy(own_half(tok, h), TOK.at[block(gx, q, h)], loc.at[2 + h]))
        local.append(pltpu.make_async_copy(own_half(cot, h), COT.at[block(gx, q, h)], loc.at[4 + h]))
    local.append(pltpu.make_async_copy(cot, OWN, loc.at[7]))

    def fc1_pieces(ox, oq):
        for b in range(d.ng):
            f = ((b // d.n_zp * 2 + ox) * d.n_zp + b % d.n_zp) * 4 + oq
            yield (wfc1.at[:, rows_at(f * d.r2, d.r2)],
                   WF1.at[gy, gx, zp, own_rows, pl.ds(b * d.r2, d.r2)])

    def qkv_pieces(rank):
        for k in range(3):
            yield (wqkv.at[:, rows_at(k * W + rank * 128, 128)],
                   WQ.at[gy, gx, zp, own_rows, pl.ds(k * 128, 128)])

    for i in range(1, 8):
        other = lax.rem(me.rank + i, 8)
        ox, oq = other // 4, lax.rem(other, 4)
        dev = place(gy, ox, zp, oq)
        for src, dst in qkv_pieces(other):
            remote(src, dst, w1s.at[0, other], w1r.at[0, me.rank], dev).start()
        go(remote(sm, SM.at[gy, gx, zp, q], w1s.at[2, other], w1r.at[2, me.rank], dev))
    for src, dst in qkv_pieces(me.rank):
        pltpu.make_async_copy(src, dst, w1r.at[0, me.rank]).start()
    for h in range(2):
        first(TOKS, h)
    for copy in local:
        copy.start()
    for i in range(1, 8):
        other = lax.rem(me.rank + i, 8)
        ox, oq = other // 4, lax.rem(other, 4)
        for src, dst in fc1_pieces(ox, oq):
            remote(src, dst, w1s.at[1, other], w1r.at[1, me.rank], place(gy, ox, zp, oq)).start()
    for src, dst in fc1_pieces(gx, q):
        pltpu.make_async_copy(src, dst, w1r.at[1, me.rank]).start()
    def w1_region(buf, ox, oq):
        return buf.at[gy, ox, zp, rows_at(oq * d.r1, d.r1)]

    def wait_w1(k, buf):
        for i in range(1, 8):
            other = lax.rem(me.rank + i, 8)
            dst = w1_region(buf, other // 4, lax.rem(other, 4))
            remote(dst, dst, w1s.at[k, other], w1r.at[k, other], x_dev).wait_recv()
        dst = w1_region(buf, gx, q)
        pltpu.make_async_copy(dst, dst, w1r.at[k, me.rank]).wait()

    for copy in local:
        copy.wait()
    wait_w1(0, WQ)
    for i in range(1, 8):
        other = lax.rem(me.rank + i, 8)
        dst = SM.at[gy, other // 4, zp, lax.rem(other, 4)]
        remote(sm, dst, w1s.at[2, other], w1r.at[2, other], x_dev).wait_recv()
    go(remote(SM.at[gy, :, zp], SM.at[gy, :, zp], zs.at[2], zr.at[2], zz_dev))
    go(remote(WQ.at[gy, :, zp], WQ.at[gy, :, zp], zs.at[0], zr.at[0], zz_dev))
    for h in range(2):
        second(TOKS, h)
    wait_w1(1, WF1)
    go(remote(WF1.at[gy, :, zp], WF1.at[gy, :, zp], zs.at[1], zr.at[1], zz_dev))
    for h in range(2):
        relay_first(TOKS, h)
    go(remote(wf2, WF2.at[gy, zp], zs.at[3], zr.at[3], zz_dev))
    for h in range(2):
        first(COTS, h)
    for h in range(2):
        second(COTS, h)
    per = 128 // d.r1
    owner = me.f // per
    part = lax.rem(me.f, per)
    wx, wq = owner // 4, lax.rem(owner, 4)
    wo_mine = jnp.logical_and(wx == gx, wq == q)
    wo_dst = WO.at[rows_at(part * d.r1, d.r1)]
    wo_own = remote(wo, wo_dst, os_.at[0], or_.at[part], place(gy, wx, zp, wq))
    wo_here = pltpu.make_async_copy(wo, wo_dst, loc.at[6])
    for i in range(1, d.ng):
        group = lax.rem(gy * d.n_zp + zp + i, d.ng)
        go(remote(wo, wo_dst, os_.at[i], or_.at[part],
                  place(group // d.n_zp, wx, lax.rem(group, d.n_zp), wq)))

    @pl.when(wo_mine)
    def _():
        wo_here.start()

    @pl.when(jnp.logical_not(wo_mine))
    def _():
        wo_own.start()

    remote(SM.at[gy, :, oz], SM.at[gy, :, oz], zs.at[2], zr.at[2], zz_dev).wait_recv()
    go(remote(SM.at[gy], SM.at[gy], ys.at[2], yr.at[2], yy_dev))
    remote(WQ.at[gy, :, oz], WQ.at[gy, :, oz], zs.at[0], zr.at[0], zz_dev).wait_recv()
    go(remote(WQ.at[gy], WQ.at[gy], ys.at[0], yr.at[0], yy_dev))
    for h in range(2):
        relay_second(TOKS, h)
    wait_twin(TOKS)
    remote(SM.at[oy], SM.at[oy], ys.at[2], yr.at[2], yy_dev).wait_recv()
    in_lane = lax.broadcasted_iota(jnp.int32, (8, 128), 1) // d.r1
    parts = 128 // d.r1
    for j in range(8):
        rows3 = [jnp.zeros((8, 128), F32)] * 3
        for k in range(parts):
            g_, dv = divmod(j * parts + k, d.n_dev)
            packed = SM[g_ // 2, g_ % 2, dv // 4, dv % 4].astype(F32)[0:8]
            for v in range(3):
                turn = (k - v) % parts * d.r1
                moved = pltpu.roll(packed, turn, 1) if turn else packed
                rows3[v] = jnp.where(in_lane == k, moved, rows3[v])
        for v in range(3):
            VEC[v : v + 1, j * 128 : (j + 1) * 128] = rows3[v][0:1]
    for b in range(d.ng):
        BF1[:, b * 128 : (b + 1) * 128] = SM[b // d.n_zp, gx, b % d.n_zp, q].astype(F32)
    SUMS[...] = jnp.zeros_like(SUMS)

    def slot_of(s):
        index = (gy * 2 + s) * d.n_zp + zp
        return lens[index], offs[index]

    def normalise(rows):
        x = rows.astype(F32)
        centred = x - jnp.mean(x, axis=-1, keepdims=True)
        inverse = lax.rsqrt(jnp.mean(centred * centred, axis=-1, keepdims=True) + 1e-5)
        return centred * inverse, inverse

    def live_column(s, first_place, n):
        length, offset = slot_of(s)
        at = lax.broadcasted_iota(jnp.int32, (n, 1), 0) + first_place
        return jnp.logical_and(at >= offset, at < offset + length)

    def live_row(s, first_place, n):
        length, offset = slot_of(s)
        at = lax.broadcasted_iota(jnp.int32, (1, n), 1) + first_place
        return jnp.logical_and(at >= offset, at < offset + length)

    @pl.loop(0, 8)
    def _(i):
        normed, _ = normalise(TOK[rows_at(i * R, R), :])
        h = (normed * VEC[0:1, :] + VEC[1:2, :]).astype(BF)
        H[rows_at(i * R, R), :] = h
        HT[:, rows_at(i * R, R)] = h.T

    relay_first(COTS, 0)
    remote(WF1.at[gy, :, oz], WF1.at[gy, :, oz], zs.at[1], zr.at[1], zz_dev).wait_recv()
    go(remote(WF1.at[gy], WF1.at[gy], ys.at[1], yr.at[1], yy_dev))
    remote(WQ.at[oy], WQ.at[oy], ys.at[0], yr.at[0], yy_dev).wait_recv()

    lane = lax.rem(lax.broadcasted_iota(jnp.int32, (1, 128), 1), 64)

    def turn_tables_of(s, t):
        _, offset = slot_of(s)
        co, so = c0[pl.ds(offset, 1), :], s0[pl.ds(offset, 1), :]
        cc, ss = c0[rows_at(t * R, R), :], s0[rows_at(t * R, R), :]
        cos = cc * co + ss * so
        sin = ss * co - cc * so
        cos = jnp.where(lane < ROT, cos, 1.0)
        sin = jnp.where(lane < ROT // 2, -sin, jnp.where(lane < ROT, sin, 0.0))
        return cos, sin

    def turned(x, cos, sin):
        other = jnp.where(lane < ROT // 2, pltpu.roll(x, 128 - ROT // 2, 1), pltpu.roll(x, ROT // 2, 1))
        return x * cos + other * sin

    wq_all = (W, d.qs)

    @pl.loop(0, 8)
    def _(i):
        s, t = i // 4, lax.rem(i, 4)
        rows = rows_at(i * R, R)
        qkv = cdot(H[rows, :], WQ[...].reshape(wq_all), 1, 0)
        cos, sin = turn_tables_of(s, t)
        query = turned(qkv[:, :128], cos, sin).astype(BF)
        Q[rows, :] = (query.astype(F32) * 0.125).astype(BF)
        key = turned(qkv[:, 128:256], cos, sin).astype(BF)
        K[rows, :] = key
        KT[:, rows] = key.T
        value = qkv[:, 256:].astype(BF)
        V[rows, :] = value
        VT[:, rows] = value.T

    relay_first(COTS, 1)
    remote(WF2.at[gy, oz], WF2.at[gy, oz], zs.at[3], zr.at[3], zz_dev).wait_recv()
    go(remote(WF2.at[gy], WF2.at[gy], ys.at[3], yr.at[3], yy_dev))
    lane128 = lax.broadcasted_iota(jnp.int32, (1, 128), 1)

    def of_head(x, j):
        keep = (lane128 < 64) if j == 0 else (lane128 >= 64)
        return jnp.where(keep, x, jnp.zeros_like(x))

    def attend(s, t):
        n = (t + 1) * R
        base = pl.multiple_of(s * S, S)
        rows = rows_at(s * S + t * R, R)
        query = Q[rows, :]
        bias = jnp.where(live_column(s, 0, n), 0.0, -1e30)
        key_at = lax.broadcasted_iota(jnp.int32, (R, R), 0)
        query_at = lax.broadcasted_iota(jnp.int32, (R, R), 1)
        for j in range(2):
            scores = cdot(K[pl.ds(base, n), :], of_head(query, j), 1, 1)
            diag = scores[t * R :] + jnp.where(key_at == query_at, 0.0, bias[t * R :])
            diag = jnp.where(key_at <= query_at, diag, -1e30)
            top = jnp.max(diag, axis=0, keepdims=True)
            if t > 0:
                left = scores[: t * R] + bias[: t * R]
                top = jnp.maximum(top, jnp.max(left, axis=0, keepdims=True))
                left = jnp.exp(left - top)
            diag = jnp.exp(diag - top)
            total = jnp.sum(diag, axis=0, keepdims=True)
            if t > 0:
                total = total + jnp.sum(left, axis=0, keepdims=True)
            scale = 1.0 / total
            prob = PT[t].at[s * 2 + j]
            prob[pl.ds(t * R, R), :] = (diag * scale).astype(BF)
            if t > 0:
                prob[pl.ds(0, t * R), :] = (left * scale).astype(BF)
            out = cdot(VT[pl.ds(j * 64, 64), pl.ds(base, n)], prob[...], 1, 0)
            ATT[rows, pl.ds(j * 64, 64)] = out.T.astype(BF)
            keep = live_row(s, t * R, R)
            AT[pl.ds(d.ffs + j * 64, 64), rows] = jnp.where(keep, out, 0.0).astype(BF)

    @pl.loop(0, 2)
    def _(s):
        for t in range(4):
            attend(s, t)

    relay_second(COTS, 0)
    remote(WF1.at[oy], WF1.at[oy], ys.at[1], yr.at[1], yy_dev).wait_recv()

    @pl.loop(0, 8)
    def _(i):
        rows = rows_at(i * R, R)
        pre = cdot(H[rows, :], WF1[...].reshape((W, d.ffs)), 1, 0) + BF1[3:4, :]
        act, slope = gelu_parts(pre)
        act = act.astype(BF)
        ACT[rows, :] = act
        SG[rows, :] = slope.astype(BF)
        keep = live_column(i // 4, lax.rem(i, 4) * R, R)
        AT[pl.ds(0, d.ffs), rows] = jnp.where(keep, act, jnp.zeros_like(act)).T

    relay_second(COTS, 1)
    wait_twin(COTS)

    def over_gy(part, buf, sem):
        return remote(part.at[oy], buf, sem.at[0, 0], sem.at[1, 0], yy_dev)

    for side in (oy, gy):
        for m in range(d.c2 // 256):
            cols = pl.ds(m * 256, 256)
            out = cdot(AT[...], COT[:, rows_at(side * d.c2 + m * 256, 256)], 1, 0).astype(BF)
            GB[side, :, cols] = out
            if side is oy:
                remote(GB.at[oy, :, cols], yb.at[:, cols], bsem.at[0, 0], bsem.at[1, 0], yy_dev).start()
    sends.append(over_gy(GB, yb, bsem))
    remote(WF2.at[oy], WF2.at[oy], ys.at[3], yr.at[3], yy_dev).wait_recv()
    for i in range(per):
        source = me.rank * per + i
        dst = WO.at[pl.ds(i * d.r1, d.r1)]

        @pl.when(source != me.f)
        def _():
            remote(wo, dst, os_.at[0], or_.at[i], x_dev).wait_recv()

    @pl.when(wo_mine)
    def _():
        wo_here.wait()

    def to_twin(src, t_buf, k, s, t):
        h = t // 2
        bz = jnp.where(t < 2, t, 3 - t)
        pb = 2 * t + jnp.where(t < 2, 1 - c, c)
        n = (s * 2 + bz) * 2 + h
        remote(src.at[rows_at(s * S + pb * half, half)], t_buf.at[s, bz, h], tsem.at[k, 0, n],
               tsem.at[k, 1, n], c_dev).start()

    def twin_blocks(src, t_buf, k):
        for bx in range(2):
            for bz in range(2):
                for h in range(2):
                    n = (bx * 2 + bz) * 2 + h
                    own = src.at[block(bx, bz * 2 + c, h)]
                    copy = remote(own, t_buf.at[bx, bz, h], tsem.at[k, 0, n], tsem.at[k, 1, n], c_dev)
                    yield bx, bz, h, own, copy

    def add_twin(src, t_buf, k):
        for bx, bz, h, own, copy in twin_blocks(src, t_buf, k):
            copy.wait_recv()
            t_buf[bx, bz, h] = (t_buf[bx, bz, h].astype(F32) + own[...].astype(F32)).astype(BF)

    def twin_sent(src, t_buf, k):
        for _, _, _, _, copy in twin_blocks(src, t_buf, k):
            copy.wait_send()

    def block_of(h, part):
        mine = zl if h == 0 else gx
        return 1 - mine if part == 0 else mine

    def hop_one(t_buf, b2, k, h, part):
        b, n = block_of(h, part), 8 + h * 2 + part
        src, dev = (t_buf.at[1 - gx, b, 0], x_dev) if h == 0 else (t_buf.at[b, 1 - zl, 1], z_dev)
        return remote(src, b2.at[h, b], tsem.at[k, 0, n], tsem.at[k, 1, n], dev)

    def add_one(t_buf, b2, k, h, part):
        hop_one(t_buf, b2, k, h, part).wait_recv()
        b = block_of(h, part)
        own = t_buf[gx, b, 0] if h == 0 else t_buf[b, zl, 1]
        b2[h, b] = (b2[h, b].astype(F32) + own.astype(F32)).astype(BF)

    def hop_two(b2, b3, k, h):
        src, dev = (b2.at[0, 1 - zl], z_dev) if h == 0 else (b2.at[1, 1 - gx], x_dev)
        return remote(src, b3.at[h], tsem.at[k, 0, 12 + h], tsem.at[k, 1, 12 + h], dev)

    def rows_of(b2, b3, h):
        return b2[h, zl if h == 0 else gx].astype(F32) + b3[h].astype(F32)


    wf2_all = (d.ffs, W)

    @pl.loop(0, 8)
    def _(i):
        rows = rows_at(i * R, R)
        mix = cdot(ATT[rows, :], WO[...], 1, 0) + cdot(ACT[rows, :], WF2[...].reshape(wf2_all), 1, 0)
        MIXP[rows, :] = mix.astype(BF)
        to_twin(MIXP, mt, 0, i // 4, lax.rem(i, 4))

    @pl.loop(0, 8)
    def _(i):
        rows = rows_at(i * R, R)
        keep = live_column(i // 4, lax.rem(i, 4) * R, R)
        grad = COT[rows, :]
        grad = jnp.where(keep, grad, jnp.zeros_like(grad))
        grad_act = cdot(grad, WF2[...].reshape(wf2_all), 1, 1)
        grad_pre = (grad_act * SG[rows, :].astype(F32)).astype(BF)
        SG[rows, :] = grad_pre
        GATT[rows, :] = cdot(grad, WO[...], 1, 1).astype(BF)
        SUMS[2:3, :] += jnp.sum(grad.astype(F32), axis=0, keepdims=True)
        SUMS[3:4, : d.ffs] += jnp.sum(grad_pre.astype(F32), axis=0, keepdims=True)

    add_twin(MIXP, mt, 0)
    for part in range(2):
        for h in range(2):
            go(hop_one(mt, m2, 0, h, part))

    @pl.loop(0, d.ffs // 256)
    def _(n):
        cols = rows_at(n * 256, 256)
        out = cdot(HT[...], SG[:, cols], 1, 0).astype(BF).reshape(8, 2, d.rdg, 256)
        GA[0, :, :, cols] = out[:, 0]
        GA[1, :, :, cols] = out[:, 1]
        remote(GA.at[oy, :, :, cols], ya.at[:, :, cols], asem.at[0, 0], asem.at[1, 0], yy_dev).start()

    sends.append(over_gy(GA, ya, asem))
    def y_sum(part, buf, sem, count):
        over_gy(part, buf, sem).wait_recv()
        for b in range(count):
            buf[b] = (buf[b].astype(F32) + part[gy, b].astype(F32)).astype(BF)

    over_gy(GB, yb, bsem).wait_recv()
    for b in range(5):
        rr = pl.ds(b * 128, 128)
        yb[rr, :] = (yb[rr, :].astype(F32) + GB[gy, rr, :].astype(F32)).astype(BF)
    b_rows = d.n_zp * d.r2
    f2_over_zp = remote(yb.at[rows_at(oz * b_rows, b_rows)], zb.at[pl.ds(0, b_rows)],
                        bsem.at[0, 1], bsem.at[1, 1], zz_dev)
    go(f2_over_zp)
    wo_zp = me.rank * d.n_zp // 8
    wo_over_zp = remote(yb.at[pl.ds(d.ffs, 128)], zb.at[pl.ds(b_rows, 128)],
                        bsem.at[0, 2], bsem.at[1, 2], zz_dev)

    @pl.when(wo_zp != zp)
    def _():
        wo_over_zp.start()

    def attend_back(s, t):
        n = (t + 1) * R
        base = pl.multiple_of(s * S, S)
        rows = rows_at(s * S + t * R, R)
        query, grad = Q[rows, :], GATT[rows, :]
        cos, sin = turn_tables_of(s, t)
        halves = []
        for j in range(2):
            grad_j = of_head(grad, j)
            prob_low = PT[t][s * 2 + j]
            grad_prob = cdot(V[pl.ds(base, n), :], grad_j, 1, 1)
            prob = prob_low.astype(F32)
            both = prob * grad_prob
            inner = jnp.sum(both, axis=0, keepdims=True)
            score = (both - prob * inner).astype(BF)
            DV[pl.ds(0, n), :] += cdot(prob_low, grad_j, 1, 0)
            DK[pl.ds(0, n), :] += cdot(score, of_head(query, j), 1, 0)
            halves.append(cdot(KT[pl.ds(j * 64, 64), pl.ds(base, n)], score, 1, 0))
        grad_q = jnp.concatenate(halves, axis=0).T * 0.125
        GQKV[rows, 0:128] = turned(grad_q, cos, -sin).astype(BF)

    @pl.loop(0, 2)
    def _(s):
        DK[...] = jnp.zeros_like(DK)
        DV[...] = jnp.zeros_like(DV)
        for t in range(4):
            attend_back(s, t)
        for t in range(4):
            rows = rows_at(s * S + t * R, R)
            cos, sin = turn_tables_of(s, t)
            GQKV[rows, 128:256] = turned(DK[pl.ds(t * R, R), :], cos, -sin).astype(BF)
            GQKV[rows, 256:384] = DV[pl.ds(t * R, R), :].astype(BF)

    out = cdot(HT[...], GQKV[...], 1, 0).astype(BF).reshape(8, 2, d.rdg, d.qs)
    GQ[0] = out[:, 0]
    GQ[1] = out[:, 1]
    go(over_gy(GQ, yq, qsem))
    for h in range(2):
        add_one(mt, m2, 0, h, 0)
        go(hop_two(m2, m3, 0, h))
    for h in range(2):
        add_one(mt, m2, 0, h, 1)
    y_sum(GA, ya, asem, 8)
    f1_over_zp = remote(ya.at[pl.ds(oz * 4, 4)], za, asem.at[0, 1], asem.at[1, 1], zz_dev)
    go(f1_over_zp)


    f2_over_zp.wait_recv()
    for b in range(d.n_zp):
        rr = pl.ds(b * 128, 128)
        own = yb[rows_at(zp * b_rows + b * 128, 128), :]
        zb[rr, :] = (zb[rr, :].astype(F32) + own.astype(F32)).astype(BF)
    f2_cols = rows_at(gy * d.c2, d.c2)
    f2_mine = F2.at[rows_at(q * 128, 128), f2_cols]

    def f2_copies():
        for j in range(2):
            for ox in range(2):
                away = jnp.logical_not(jnp.logical_and(ox == gx, gx * 2 + j == q))
                src = zb.at[pl.ds(j * 128, 128)]
                yield away, src, remote(src, f2_mine, dsem.at[0, 0, j * 2 + ox], dsem.at[0, 1, q],
                                        place(gy, ox, zp, gx * 2 + j))

    for away, src, copy in f2_copies():
        here = pltpu.make_async_copy(src, f2_mine, dsem.at[0, 2, 0])

        @pl.when(away)
        def _():
            copy.start()

        @pl.when(jnp.logical_not(away))
        def _():
            here.start()
            here.wait()

    wo_src = zb.at[pl.ds(b_rows, 128)]
    wo_final = remote(wo_src, FWO.at[:, f2_cols], dsem.at[1, 0, 0], dsem.at[1, 1, 0], x_dev)
    wo_stay = pltpu.make_async_copy(wo_src, FWO.at[:, f2_cols], dsem.at[1, 2, 0])

    @pl.when(wo_zp == zp)
    def _():
        wo_over_zp.wait_recv()
        rr = pl.ds(b_rows, 128)
        zb[rr, :] = (zb[rr, :].astype(F32) + yb[pl.ds(d.ffs, 128), :].astype(F32)).astype(BF)
        wo_final.start()
        wo_stay.start()
        wo_stay.wait()

    for copy in cot_sends:
        copy.wait_send()

    @pl.loop(0, 8)
    def _(i):
        rows = rows_at(i * R, R)
        grad = cdot(SG[rows, :], WF1[...].reshape((W, d.ffs)), 1, 1)
        grad = grad + cdot(GQKV[rows, :], WQ[...].reshape(wq_all), 1, 1)
        normed, _ = normalise(TOK[rows, :])
        SUMS[0:1, :] += jnp.sum(grad * normed, axis=0, keepdims=True)
        SUMS[1:2, :] += jnp.sum(grad, axis=0, keepdims=True)
        COT[rows, :] = grad.astype(BF)
        to_twin(COT, ht, 1, i // 4, lax.rem(i, 4))

    for sq in range(4):
        away = jnp.logical_not(jnp.logical_and(gx == zl, sq == q))

        @pl.when(away)
        def _():
            remote(zb.at[pl.ds(0, 128)], F2.at[rows_at(sq * 128, 128), f2_cols], dsem.at[0, 0, 0],
                   dsem.at[0, 1, sq], x_dev).wait_recv()

    @pl.when(wo_zp != zp)
    def _():
        wo_final.wait_recv()

    go(remote(F2.at[:, f2_cols], F2.at[:, f2_cols], bsem.at[0, 3], bsem.at[1, 3], yy_dev))
    go(remote(FWO.at[:, f2_cols], FWO.at[:, f2_cols], bsem.at[0, 4], bsem.at[1, 4], yy_dev))
    add_twin(COT, ht, 1)
    for h in range(2):
        go(hop_one(ht, h2, 1, h, 0))
    SMG[...] = jnp.zeros_like(SMG)
    first_rank = jnp.where(me.rank == 0, 1.0, 0.0)
    for dd in range(d.n_dev):
        for k in range(3):
            piece = SUMS[k : k + 1, dd * 128 : (dd + 1) * 128]
            SMG[dd % 4, dd // 4, k : k + 1, :] = piece * first_rank if k == 2 else piece
    for b in range(d.ng):
        dq = gx * 2 + b % d.n_zp
        SMG[dq, b // d.n_zp, pl.ds(3 + q, 1), :] = SUMS[3:4, b * 128 : (b + 1) * 128]
    for i in range(1, 8):
        other = lax.rem(me.rank + i, 8)
        go(remote(SMG.at[lax.rem(other, 4)], s1.at[me.rank], ssem.at[0, 0, other],
                  ssem.at[0, 1, me.rank], place(gy, other // 4, zp, lax.rem(other, 4))))
    f_rows = rows_at(gy * d.rdg, d.rdg)

    def f1_pieces():
        for b in range(d.ng):
            f = ((b // d.n_zp * 2 + gx) * d.n_zp + b % d.n_zp) * 4 + q
            yield b, F1.at[f_rows, rows_at(f * 128, 128)]

    def fq_pieces():
        for k in range(3):
            yield k, FQ.at[f_rows, rows_at(k * W + me.rank * 128, 128)]

    def finish(done, mine, pieces, k):
        for b in range(4):
            done[b] = (done[b].astype(F32) + mine[zp * 4 + b].astype(F32)).astype(BF)
        for i in range(1, 8):
            other = lax.rem(me.rank + i, 8)
            ox, oq = other // 4, lax.rem(other, 4)
            for n, dst in pieces():
                remote(done.at[oq, :, pl.ds(n * 128, 128)], dst, dsem.at[k, 0, other],
                       dsem.at[k, 1, me.rank], place(gy, ox, zp, oq)).start()
        for n, dst in pieces():
            pltpu.make_async_copy(done.at[q, :, pl.ds(n * 128, 128)], dst, dsem.at[k, 2, 0]).start()
        pltpu.make_async_copy(done.at[0], done.at[0], dsem.at[k, 2, 0]).wait()

    def finished(done, k):
        for i in range(1, 8):
            other = lax.rem(me.rank + i, 8)
            remote(done.at[0], done.at[0], dsem.at[k, 0, other], dsem.at[k, 1, other],
                   x_dev).wait_recv()

    def finish_sent(done, k):
        for i in range(1, 8):
            other = lax.rem(me.rank + i, 8)
            remote(done.at[0], done.at[0], dsem.at[k, 0, other], dsem.at[k, 1, other],
                   x_dev).wait_send()

    y_sum(GQ, yq, qsem, 8)
    fq_over_zp = remote(yq.at[pl.ds(oz * 4, 4)], zq, qsem.at[0, 1], qsem.at[1, 1], zz_dev)
    go(fq_over_zp)
    f1_over_zp.wait_recv()
    finish(za, ya, f1_pieces, 2)
    for h in range(2):
        go(hop_one(ht, h2, 1, h, 1))
    for h in range(2):
        hop_two(m2, m3, 0, h).wait_recv()
        first_place = (q if h == 0 else 7 - q) * half
        rr = pl.ds(h * half, half)
        total = rows_of(m2, m3, h) + VEC[2:3, :]
        total = total + TOK[block(gx, q, h), :].astype(F32)
        MIXED[rr, :] = jnp.where(live_column(gx, first_place, half), total, 0.0).astype(BF)
    for h in range(2):
        add_one(ht, h2, 1, h, 0)
        go(hop_two(h2, h3, 1, h))
    fq_over_zp.wait_recv()
    finish(zq, yq, fq_pieces, 3)
    finished(za, 2)
    go(remote(F1.at[f_rows], F1.at[f_rows], asem.at[0, 2], asem.at[1, 2], yy_dev))
    for h in range(2):
        add_one(ht, h2, 1, h, 1)
    for i in range(1, 8):
        other = lax.rem(me.rank + i, 8)
        remote(SMG.at[0], s1.at[other], ssem.at[0, 0, other], ssem.at[0, 1, other],
               x_dev).wait_recv()
    s1[me.rank] = SMG[q]
    total = s1[0]
    for i in range(1, 8):
        total = total + s1[i]
    s2[d.ng] = total
    own_group = gy * d.n_zp + zp
    for i in range(1, d.ng):
        group = lax.rem(own_group + i, d.ng)
        to_z = lax.rem(group, d.n_zp)
        go(remote(s2.at[d.ng, to_z], s2.at[own_group, 0], ssem.at[1, 0, group],
                  ssem.at[1, 1, own_group], place(group // d.n_zp, gx, to_z, q)))
    finished(zq, 3)
    go(remote(FQ.at[f_rows], FQ.at[f_rows], qsem.at[0, 2], qsem.at[1, 2], yy_dev))
    for h in range(2):
        hop_two(h2, h3, 1, h).wait_recv()
        first_place = (q if h == 0 else 7 - q) * half
        rr = pl.ds(h * half, half)
        normed, inverse = normalise(TOK[block(gx, q, h), :])
        scaled = rows_of(h2, h3, h) * VEC[0:1, :]
        grad = inverse * (
            scaled
            - jnp.mean(scaled, axis=-1, keepdims=True)
            - normed * jnp.mean(scaled * normed, axis=-1, keepdims=True)
        )
        own = jnp.where(live_column(gx, first_place, half), OWN[rr, :].astype(F32), 0.0)
        TGRAD[rr, :] = (own + grad).astype(BF)
    for i in range(1, d.ng):
        group = lax.rem(own_group + i, d.ng)
        remote(s2.at[d.ng, 0], s2.at[group, 0], ssem.at[1, 0, group], ssem.at[1, 1, group],
               x_dev).wait_recv()
    total = s2[d.ng, zp]
    for i in range(1, d.ng):
        total = total + s2[lax.rem(own_group + i, d.ng), 0]
    FSM[...] = total
    o_rows, o_cols = rows_at(oy * d.rdg, d.rdg), rows_at(oy * d.c2, d.c2)
    remote(F2.at[:, o_cols], F2.at[:, o_cols], bsem.at[0, 3], bsem.at[1, 3], yy_dev).wait_recv()
    remote(FWO.at[:, o_cols], FWO.at[:, o_cols], bsem.at[0, 4], bsem.at[1, 4], yy_dev).wait_recv()
    remote(F1.at[o_rows], F1.at[o_rows], asem.at[0, 2], asem.at[1, 2], yy_dev).wait_recv()
    remote(FQ.at[o_rows], FQ.at[o_rows], qsem.at[0, 2], qsem.at[1, 2], yy_dev).wait_recv()
    twin_sent(MIXP, mt, 0)
    twin_sent(COT, ht, 1)
    for copy in sends:
        copy.wait_send()
    for k, buf in enumerate((WQ, WF1)):
        for i in range(1, 8):
            other = lax.rem(me.rank + i, 8)
            dst = w1_region(buf, gx, q)
            remote(dst, dst, w1s.at[k, other], w1r.at[k, other], x_dev).wait_send()

    @pl.when(jnp.logical_not(wo_mine))
    def _():
        wo_own.wait_send()

    @pl.when(wo_zp != zp)
    def _():
        wo_over_zp.wait_send()

    @pl.when(wo_zp == zp)
    def _():
        wo_final.wait_send()

    for away, src, copy in f2_copies():

        @pl.when(away)
        def _():
            copy.wait_send()

    finish_sent(za, 2)
    finish_sent(zq, 3)


def layer(d, lens, offs, tok, cot, wqkv, wo, wfc1, wf2, sm, c0, s0):
    smem = pl.BlockSpec(memory_space=pltpu.SMEM)
    vm = pl.BlockSpec(memory_space=pltpu.VMEM)
    hbm = pl.BlockSpec(memory_space=pl.ANY)
    dma = pltpu.SemaphoreType.DMA
    shape = jax.ShapeDtypeStruct
    R, W, half = d.rows, d.width, d.rows // 2
    N = 8 * R

    def bf(*dims):
        return pltpu.VMEM(dims, BF)

    def f32(*dims):
        return pltpu.VMEM(dims, F32)

    return pl.pallas_call(
        functools.partial(layer_kernel, d),
        out_shape=(
            shape((R, W), BF),
            shape((R, W), BF),
            shape((d.rd, d.ff), BF),
            shape((d.rd, 3 * W), BF),
            shape((d.ff // d.n_dev, W), BF),
            shape((d.rd, W), BF),
            shape((8, 128), F32),
        ),
        in_specs=[smem, smem] + [hbm] * 7 + [vm] * 2,
        out_specs=(vm,) * 7,
        scratch_shapes=[
            bf(N, W), bf(N, W), bf(N, W), bf(W, N),
            bf(N, 128), bf(N, 128), bf(N, 128), bf(128, N), bf(128, N),
            bf(4, R, R), bf(4, 2 * R, R), bf(4, 3 * R, R), bf(4, 4 * R, R),
            bf(N, d.ffs), bf(d.ffs + 128, N), bf(N, d.ffs), bf(N, 128), bf(N, 128), bf(N, d.qs),
            f32(4 * R, 128), f32(4 * R, 128), bf(N, W),
            bf(d.n_gy, 2, d.n_zp, 4 * d.r1, d.ffs), bf(d.n_gy, 2, d.n_zp, 4 * d.r1, d.qs),
            bf(d.n_gy, d.n_zp, d.r2, W), bf(128, W), bf(d.n_gy, 2, d.n_zp, 4, 16, 128),
            f32(16, W), f32(16, d.ffs), f32(4, d.n_zp, 8, 128), f32(8, W), bf(R, W),
            bf(2, 2, 2, half, W), bf(2, 2, half, W), bf(2, half, W),
            bf(2, 2, 2, half, W), bf(2, 2, half, W), bf(2, half, W),
            bf(d.n_gy, d.ffs + 128, d.c2), bf(d.n_gy, 8, d.rdg, d.ffs), bf(d.n_gy, 8, d.rdg, d.qs),
            bf(d.ffs + 128, d.c2), bf(8, d.rdg, d.ffs), bf(8, d.rdg, d.qs),
            bf(d.ffs // d.n_zp + 128, d.c2), bf(4, d.rdg, d.ffs), bf(4, d.rdg, d.qs),
            f32(8, d.n_zp, 8, 128), f32(d.ng + 1, d.n_zp, 8, 128),
            dma((8,)), dma((7, 2)), dma((8, 2)), dma((7, 2)), dma((8, 2)),
            dma((3, 8)), dma((3, 8)), dma((4,)), dma((4,)), dma((4,)), dma((4,)),
            dma((d.ng,)), dma((128 // d.r1,)),
            dma((2, 2, 14)), dma((2, 5)), dma((2, 3)), dma((2, 3)), dma((2, 2, 8)), dma((4, 3, 8)),
        ],
        compiler_params=pltpu.CompilerParams(
            has_side_effects=True, vmem_limit_bytes=67043328
        ),
        name="layer",
    )(lens, offs, tok, cot, wqkv, wo, wfc1, wf2, sm, c0, s0)


def place_tables(slot):
    freq = np.exp(np.arange(ROT // 2) * (-2.0 * math.log(10000.0) / ROT))
    angle = np.arange(slot)[:, None] * freq[np.arange(128) % (ROT // 2)][None]
    return np.cos(angle).astype(np.float32), np.sin(angle).astype(np.float32)


def small_pack(d, ln_gain, ln_bias, b_fc1, b_fc2):
    gap = jnp.zeros((3 * 128 - 3 * d.r1,), BF)
    rest = jnp.zeros((12 * 128,), BF)
    return jnp.concatenate([ln_gain, ln_bias, b_fc2, gap, b_fc1, rest]).reshape(16, 128)


def local_one(d, tokens, cotangent, lengths, offsets, ln_gain, ln_bias, w_qkv, w_out, w_fc1, b_fc1,
              w_fc2, b_fc2):
    sm = small_pack(d, ln_gain, ln_bias, b_fc1, b_fc2)
    c0, s0 = place_tables(4 * d.rows)
    mixed, token_grad, f1, fq, f2, fwo, small = layer(
        d, lengths, offsets, tokens, cotangent, w_qkv, w_out, w_fc1, w_fc2, sm,
        jnp.asarray(c0), jnp.asarray(s0),
    )
    per = d.rd
    return (mixed, token_grad, small[0, :per], small[1, :per], fq.astype(F32), fwo.astype(F32),
            f1.astype(F32), small[3:7].reshape(-1), f2.astype(F32), small[2, :per])


def solution(mesh):
    rows = ("grp", "dev")

    def program(*args):
        tokens, w_fc1 = args[0], args[8]
        n = mesh.shape["grp"] * mesh.shape["dev"]
        d = Dims(mesh, tokens.shape[0] // n, tokens.shape[1], w_fc1.shape[1])
        whole_tiles = d.n_gy == 2 and d.r2 == 128 and d.r1 % 16 == 0 and d.rd == 128
        return jax.shard_map(
            functools.partial(local_one if whole_tiles else local, d),
            mesh=mesh,
            in_specs=(
                P(rows, None), P(rows, None), P(), P(), P(rows), P(rows), P(rows, None),
                P(rows, None), P(rows, None), P(rows), P(rows, None), P(rows),
            ),
            out_specs=(
                P(rows, None), P(rows, None), P("dev"), P("dev"), P("dev", None), P("dev", None),
                P("dev", None), P("dev"), P("dev", None), P("dev"),
            ),
            check_vma=False,
        )(*args)

    return program
```

time: 800 us -> 202 us (0.25); the launches traced: 791 us -> 202 us
  waiting for transfers between devices: 463 us -> 0 us
  Pallas kernels: 0 us -> 187 us
  blocking collectives: 111 us -> 0 us
  matrix products: 92.7 us -> 0 us
  local copies, waits for them, and re-layouts: 60.8 us -> 7.54 us
  other arithmetic: 43.1 us -> 6.46 us
  between operations: 18 us -> 0.68 us
    ppermute x4 -> x0, waiting for transfers between devices: 248 us -> none  [swapped(): lax.ppermute(array, axis, [(i, i ^ 1 << distance) for i in range(lax.axis...]
    pallas_call x0 -> x1, Pallas kernels: none -> 187 us  [layer(): pl.pallas_call(functools.partial(layer_kernel, d), out_shape=(shape((R, W...]
    reduce_scatter x4 -> x0, waiting for transfers between devices: 115 us -> none  [the longest x1 81.2 us: local(): lax.psum_scatter(gradients[2].astype(jnp.bfloat16), 'dev', scatter_dimens...]
    dot_general x36 -> x0, matrix products: 92.7 us -> none  [the longest x4 8.95 us: attend_backward(): jnp.einsum('hqk,qhd->khd', probs_low, part_grad, preferred_element_type=j...]
    unnamed x2 -> x0, blocking collectives: 62.5 us -> none
    all_gather x4 -> x0, waiting for transfers between devices: 61.3 us -> none  [the longest x1 38.2 us: local(): lax.all_gather(w_fc2, ('grp', 'dev'), axis=0, tiled=True)]
    all_gather x1 -> x0, blocking collectives: 40 us -> none  [local(): lax.all_gather(b_fc1, ('grp', 'dev'), axis=0, tiled=True)]
    psum x1 -> x0, waiting for transfers between devices: 35.7 us -> none  [local(): lax.psum(shares[2].astype(jnp.bfloat16), 'grp').astype(jnp.float32)]
  transfers between devices with their start and end apart: 13 -> 0, of which waited for: 8 -> 0; matrix products, arithmetic and copies ran while one was open for 21% -> 0% of each run, Pallas kernels for 0% -> 0%
where the time goes in v1:
time: 202 us
  Pallas kernels  187 us (93%)
  local copies, waits for them, and re-layouts  7.54 us (4%)
  other arithmetic  6.46 us (3%)
    pallas_call x1, Pallas kernels, layer(): pl.pallas_call(functools.partial(layer_kernel, d), out_shape=(shape((R, W...  187 us

profile of v1, /device:TPU:9, one launch (start us, length us, event | category | flops | bytes accessed | tf_op | source)
XLA Modules:
  0.0 201.6 jit_solution(14226654022997112007)
XLA Ops:
  0.7 3.3 %concatenate.3 = bf16[2048]{0:T(1024)(128)(2,1)} concatenate(bf16[32]{0:T(256)(128)(2,1)} %param.18, bf16[32]{0:T(256)(128)(2,1)} %param.19, bf16[32]{0:T(256)(128)(2,1)} %param.25, bf16[288]{0:T(512)(128)(2,1)S(1)} %broadcast_in_dim.6, bf16[128]{0:T(256)(128)(2,1)} %param.23, bf16[1536]{0:T(1024)(128)(2,1)S(1)} %broadcast_in_dim.7), dimensions={0} | concatenate | bytes 8192 | tf_op jit(solution)/shard_map/concatenate | solution.py:1465
  4.0 186.9 %layer.1 = (bf16[256,1024]{1,0:T(8,128)(2,1)}, bf16[256,1024]{1,0:T(8,128)(2,1)}, bf16[128,4096]{1,0:T(8,128)(2,1)}, bf16[128,3072]{1,0:T(8,128)(2,1)}, bf16[512...) custom-call(s32[8]{0:T(128)} %lens.1, s32[8]{0:T(128)} %offs.1, bf16[256,1024]{1,0:T(8,128)(2,1)} %tok.1, ...), custom_call_target="tpu_custom_call" | custom-call | tf_op jit(solution)/shard_map/layer/pallas_call | solution.py:1416
  190.9 0.0 copy-start
  190.9 1.3 slice_bitcast_fusion.1
  192.2 1.3 slice_bitcast_fusion
  193.5 2.8 %convert_element_type.14 = f32[128,4096]{1,0:T(8,128)} convert(bf16[128,4096]{1,0:T(8,128)(2,1)} %get-tuple-element.22) | non-fusion elementwise | flops 524288 | bytes 3145728 | tf_op jit(solution)/shard_map/convert_element_type | solution.py:1478
  196.2 0.0 copy-start.1
  196.3 0.0 copy-done
  196.3 0.0 copy-start.4
  196.3 1.6 convert_element_type.15
  197.8 0.0 copy-start.3
  197.8 0.0 copy-done.1
  197.8 0.0 copy-start.2
  197.8 1.3 convert_element_type.12
  199.1 0.0 copy-done.4
  199.1 0.8 convert_element_type.13
  200.0 0.0 copy-done.3
  200.0 0.8 copy.26
  200.8 0.0 copy-done.2
  200.8 0.8 copy.27
  (2 shorter events, 0.0 us)
Async XLA Ops:
  190.9 5.4 %copy-start = (bf16[512,1024]{1,0:T(8,128)(2,1)S(1)}, bf16[512,1024]{1,0:T(8,128)(2,1)}, u32[]{:S(2)}) copy-start(bf16[512,1024]{1,0:T(8,128)(2,1)} %get-tuple-element.23) | copy-start | bytes 3145732
  196.2 1.6 copy-start.1
  196.3 2.9 %copy-start.4 = (bf16[128,1024]{1,0:T(8,128)(2,1)S(1)}, bf16[128,1024]{1,0:T(8,128)(2,1)}, u32[]{:S(2)}) copy-start(bf16[128,1024]{1,0:T(8,128)(2,1)} %get-tuple-element.21) | copy-start | bytes 786436
  197.8 2.2 %copy-start.3 = (bf16[256,1024]{1,0:T(8,128)(2,1)S(1)}, bf16[256,1024]{1,0:T(8,128)(2,1)}, u32[]{:S(2)}) copy-start(bf16[256,1024]{1,0:T(8,128)(2,1)} %get-tuple-element.37) | copy-start | bytes 1572868
  197.8 2.9 %copy-start.2 = (bf16[256,1024]{1,0:T(8,128)(2,1)S(1)}, bf16[256,1024]{1,0:T(8,128)(2,1)}, u32[]{:S(2)}) copy-start(bf16[256,1024]{1,0:T(8,128)(2,1)} %get-tuple-element.38) | copy-start | bytes 1572868

commit v2 on v1

--- a/solution.py
+++ b/solution.py
@@ -716,7 +716,7 @@
     TOKS, COTS = (tok, TOK, ts, tr, sends), (cot, COT, cs, cr, cot_sends)
 
     def x_first(arr, h):
-        return arr is TOKS and h == 0
+        return h == 0
 
     def own_half(src, h):
         return src.at[pl.ds(h * half, half)]
@@ -816,15 +816,31 @@
         other = lax.rem(me.rank + i, 8)
         dst = SM.at[gy, other // 4, zp, lax.rem(other, 4)]
         remote(sm, dst, w1s.at[2, other], w1r.at[2, other], x_dev).wait_recv()
-    go(remote(SM.at[gy, :, zp], SM.at[gy, :, zp], zs.at[2], zr.at[2], zz_dev))
-    go(remote(WQ.at[gy, :, zp], WQ.at[gy, :, zp], zs.at[0], zr.at[0], zz_dev))
+    def own_part(k, buf):
+        part = buf.at[gy, :, zp]
+        go(remote(part, part, zs.at[k], zr.at[k], zz_dev))
+        go(remote(part, part, ys.at[k], yr.at[k], yy_dev))
+
+    def far_part(k, buf):
+        part = buf.at[gy, :, oz]
+        remote(part, part, zs.at[k], zr.at[k], zz_dev).wait_recv()
+        go(remote(part, part, ys.at[4 + k], yr.at[4 + k], yy_dev))
+
+    def complete(k, buf):
+        for part, n in ((zp, k), (oz, 4 + k)):
+            dst = buf.at[oy, :, part]
+            remote(dst, dst, ys.at[n], yr.at[n], yy_dev).wait_recv()
+
+    own_part(2, SM)
+    own_part(0, WQ)
     for h in range(2):
         second(TOKS, h)
     wait_w1(1, WF1)
-    go(remote(WF1.at[gy, :, zp], WF1.at[gy, :, zp], zs.at[1], zr.at[1], zz_dev))
+    own_part(1, WF1)
     for h in range(2):
         relay_first(TOKS, h)
     go(remote(wf2, WF2.at[gy, zp], zs.at[3], zr.at[3], zz_dev))
+    go(remote(wf2, WF2.at[gy, zp], ys.at[3], yr.at[3], yy_dev))
     for h in range(2):
         first(COTS, h)
     for h in range(2):
@@ -837,27 +853,12 @@
     wo_dst = WO.at[rows_at(part * d.r1, d.r1)]
     wo_own = remote(wo, wo_dst, os_.at[0], or_.at[part], place(gy, wx, zp, wq))
     wo_here = pltpu.make_async_copy(wo, wo_dst, loc.at[6])
-    for i in range(1, d.ng):
-        group = lax.rem(gy * d.n_zp + zp + i, d.ng)
-        go(remote(wo, wo_dst, os_.at[i], or_.at[part],
-                  place(group // d.n_zp, wx, lax.rem(group, d.n_zp), wq)))
-
-    @pl.when(wo_mine)
-    def _():
-        wo_here.start()
-
-    @pl.when(jnp.logical_not(wo_mine))
-    def _():
-        wo_own.start()
-
-    remote(SM.at[gy, :, oz], SM.at[gy, :, oz], zs.at[2], zr.at[2], zz_dev).wait_recv()
-    go(remote(SM.at[gy], SM.at[gy], ys.at[2], yr.at[2], yy_dev))
-    remote(WQ.at[gy, :, oz], WQ.at[gy, :, oz], zs.at[0], zr.at[0], zz_dev).wait_recv()
-    go(remote(WQ.at[gy], WQ.at[gy], ys.at[0], yr.at[0], yy_dev))
+    far_part(2, SM)
+    far_part(0, WQ)
     for h in range(2):
         relay_second(TOKS, h)
     wait_twin(TOKS)
-    remote(SM.at[oy], SM.at[oy], ys.at[2], yr.at[2], yy_dev).wait_recv()
+    complete(2, SM)
     in_lane = lax.broadcasted_iota(jnp.int32, (8, 128), 1) // d.r1
     parts = 128 // d.r1
     for j in range(8):
@@ -903,9 +904,21 @@
         HT[:, rows_at(i * R, R)] = h.T
 
     relay_first(COTS, 0)
-    remote(WF1.at[gy, :, oz], WF1.at[gy, :, oz], zs.at[1], zr.at[1], zz_dev).wait_recv()
-    go(remote(WF1.at[gy], WF1.at[gy], ys.at[1], yr.at[1], yy_dev))
-    remote(WQ.at[oy], WQ.at[oy], ys.at[0], yr.at[0], yy_dev).wait_recv()
+    far_part(1, WF1)
+    for i in range(1, d.ng):
+        group = lax.rem(gy * d.n_zp + zp + i, d.ng)
+        go(remote(wo, wo_dst, os_.at[i], or_.at[part],
+                  place(group // d.n_zp, wx, lax.rem(group, d.n_zp), wq)))
+
+    @pl.when(wo_mine)
+    def _():
+        wo_here.start()
+
+    @pl.when(jnp.logical_not(wo_mine))
+    def _():
+        wo_own.start()
+
+    complete(0, WQ)
 
     lane = lax.rem(lax.broadcasted_iota(jnp.int32, (1, 128), 1), 64)
 
@@ -942,7 +955,7 @@
 
     relay_first(COTS, 1)
     remote(WF2.at[gy, oz], WF2.at[gy, oz], zs.at[3], zr.at[3], zz_dev).wait_recv()
-    go(remote(WF2.at[gy], WF2.at[gy], ys.at[3], yr.at[3], yy_dev))
+    go(remote(WF2.at[gy, oz], WF2.at[gy, oz], ys.at[7], yr.at[7], yy_dev))
     lane128 = lax.broadcasted_iota(jnp.int32, (1, 128), 1)
 
     def of_head(x, j):
@@ -986,7 +999,7 @@
             attend(s, t)
 
     relay_second(COTS, 0)
-    remote(WF1.at[oy], WF1.at[oy], ys.at[1], yr.at[1], yy_dev).wait_recv()
+    complete(1, WF1)
 
     @pl.loop(0, 8)
     def _(i):
@@ -1013,7 +1026,9 @@
             if side is oy:
                 remote(GB.at[oy, :, cols], yb.at[:, cols], bsem.at[0, 0], bsem.at[1, 0], yy_dev).start()
     sends.append(over_gy(GB, yb, bsem))
-    remote(WF2.at[oy], WF2.at[oy], ys.at[3], yr.at[3], yy_dev).wait_recv()
+    for part, n in ((zp, 3), (oz, 7)):
+        dst = WF2.at[oy, part]
+        remote(dst, dst, ys.at[n], yr.at[n], yy_dev).wait_recv()
     for i in range(per):
         source = me.rank * per + i
         dst = WO.at[pl.ds(i * d.r1, d.r1)]
@@ -1442,7 +1457,7 @@
             bf(d.ffs // d.n_zp + 128, d.c2), bf(4, d.rdg, d.ffs), bf(4, d.rdg, d.qs),
             f32(8, d.n_zp, 8, 128), f32(d.ng + 1, d.n_zp, 8, 128),
             dma((8,)), dma((7, 2)), dma((8, 2)), dma((7, 2)), dma((8, 2)),
-            dma((3, 8)), dma((3, 8)), dma((4,)), dma((4,)), dma((4,)), dma((4,)),
+            dma((3, 8)), dma((3, 8)), dma((4,)), dma((4,)), dma((8,)), dma((8,)),
             dma((d.ng,)), dma((128 // d.r1,)),
             dma((2, 2, 14)), dma((2, 5)), dma((2, 3)), dma((2, 3)), dma((2, 2, 8)), dma((4, 3, 8)),
         ],

time: 202 us -> 200 us (0.990)
    pallas_call x1, Pallas kernels: 187 us -> 185 us  [layer(): pl.pallas_call(functools.partial(layer_kernel, d), out_shape=(shape((R, W...]
where the time goes in v2:
time: 200 us; the launch traced here: 199 us
  Pallas kernels  185 us (92%)
  local copies, waits for them, and re-layouts  7.54 us (4%)
  other arithmetic  6.46 us (3%)
    pallas_call x1, Pallas kernels, layer(): pl.pallas_call(functools.partial(layer_kernel, d), out_shape=(shape((R, W...  185 us

profile of v2, /device:TPU:9, one launch (start us, length us, event | category | flops | bytes accessed | tf_op | source)
XLA Modules:
  0.0 199.3 jit_solution(8617729518529776172)
XLA Ops:
  0.7 3.3 %concatenate.3 = bf16[2048]{0:T(1024)(128)(2,1)} concatenate(bf16[32]{0:T(256)(128)(2,1)} %param.18, bf16[32]{0:T(256)(128)(2,1)} %param.19, bf16[32]{0:T(256)(128)(2,1)} %param.25, bf16[288]{0:T(512)(128)(2,1)S(1)} %broadcast_in_dim.6, bf16[128]{0:T(256)(128)(2,1)} %param.23, bf16[1536]{0:T(1024)(128)(2,1)S(1)} %broadcast_in_dim.7), dimensions={0} | concatenate | bytes 8192 | tf_op jit(solution)/shard_map/concatenate | solution.py:1480
  4.0 184.6 %layer.1 = (bf16[256,1024]{1,0:T(8,128)(2,1)}, bf16[256,1024]{1,0:T(8,128)(2,1)}, bf16[128,4096]{1,0:T(8,128)(2,1)}, bf16[128,3072]{1,0:T(8,128)(2,1)}, bf16[512...) custom-call(s32[8]{0:T(128)} %lens.1, s32[8]{0:T(128)} %offs.1, bf16[256,1024]{1,0:T(8,128)(2,1)} %tok.1, ...), custom_call_target="tpu_custom_call" | custom-call | tf_op jit(solution)/shard_map/layer/pallas_call | solution.py:1431
  188.6 0.0 copy-start
  188.6 1.3 slice_bitcast_fusion.1
  189.9 1.3 slice_bitcast_fusion
  191.2 2.8 %convert_element_type.14 = f32[128,4096]{1,0:T(8,128)} convert(bf16[128,4096]{1,0:T(8,128)(2,1)} %get-tuple-element.22) | non-fusion elementwise | flops 524288 | bytes 3145728 | tf_op jit(solution)/shard_map/convert_element_type | solution.py:1493
  194.0 0.0 copy-start.1
  194.0 0.0 copy-done
  194.0 0.0 copy-start.4
  194.0 1.6 convert_element_type.15
  195.5 0.0 copy-start.3
  195.5 0.0 copy-done.1
  195.5 0.0 copy-start.2
  195.5 1.3 convert_element_type.12
  196.8 0.0 copy-done.4
  196.8 0.8 convert_element_type.13
  197.7 0.0 copy-done.3
  197.7 0.8 copy.26
  198.5 0.0 copy-done.2
  198.5 0.8 copy.27
  (2 shorter events, 0.0 us)
Async XLA Ops:
  188.6 5.4 %copy-start = (bf16[512,1024]{1,0:T(8,128)(2,1)S(1)}, bf16[512,1024]{1,0:T(8,128)(2,1)}, u32[]{:S(2)}) copy-start(bf16[512,1024]{1,0:T(8,128)(2,1)} %get-tuple-element.23) | copy-start | bytes 3145732
  194.0 1.6 copy-start.1
  194.0 2.9 %copy-start.4 = (bf16[128,1024]{1,0:T(8,128)(2,1)S(1)}, bf16[128,1024]{1,0:T(8,128)(2,1)}, u32[]{:S(2)}) copy-start(bf16[128,1024]{1,0:T(8,128)(2,1)} %get-tuple-element.21) | copy-start | bytes 786436
  195.5 2.2 %copy-start.3 = (bf16[256,1024]{1,0:T(8,128)(2,1)S(1)}, bf16[256,1024]{1,0:T(8,128)(2,1)}, u32[]{:S(2)}) copy-start(bf16[256,1024]{1,0:T(8,128)(2,1)} %get-tuple-element.37) | copy-start | bytes 1572868
  195.5 2.9 %copy-start.2 = (bf16[256,1024]{1,0:T(8,128)(2,1)S(1)}, bf16[256,1024]{1,0:T(8,128)(2,1)}, u32[]{:S(2)}) copy-start(bf16[256,1024]{1,0:T(8,128)(2,1)} %get-tuple-element.38) | copy-start | bytes 1572868

commit v3 on v2

--- a/solution.py
+++ b/solution.py
@@ -1187,8 +1187,6 @@
     for h in range(2):
         add_one(mt, m2, 0, h, 0)
         go(hop_two(m2, m3, 0, h))
-    for h in range(2):
-        add_one(mt, m2, 0, h, 1)
     y_sum(GA, ya, asem, 8)
     f1_over_zp = remote(ya.at[pl.ds(oz * 4, 4)], za, asem.at[0, 1], asem.at[1, 1], zz_dev)
     go(f1_over_zp)
@@ -1322,6 +1320,8 @@
     finish(za, ya, f1_pieces, 2)
     for h in range(2):
         go(hop_one(ht, h2, 1, h, 1))
+    for h in range(2):
+        add_one(mt, m2, 0, h, 1)
     for h in range(2):
         hop_two(m2, m3, 0, h).wait_recv()
         first_place = (q if h == 0 else 7 - q) * half

time: 200 us -> 200 us (level)
  no operation moved by 1% of the time
where the time goes in v3:
time: 200 us; the launch traced here: 199 us
  Pallas kernels  185 us (92%)
  local copies, waits for them, and re-layouts  7.54 us (4%)
  other arithmetic  6.46 us (3%)
    pallas_call x1, Pallas kernels, layer(): pl.pallas_call(functools.partial(layer_kernel, d), out_shape=(shape((R, W...  185 us

profile of v3, /device:TPU:9, one launch (start us, length us, event | category | flops | bytes accessed | tf_op | source)
XLA Modules:
  0.0 199.3 jit_solution(16501208029581258710)
XLA Ops:
  0.7 3.3 %concatenate.3 = bf16[2048]{0:T(1024)(128)(2,1)} concatenate(bf16[32]{0:T(256)(128)(2,1)} %param.18, bf16[32]{0:T(256)(128)(2,1)} %param.19, bf16[32]{0:T(256)(128)(2,1)} %param.25, bf16[288]{0:T(512)(128)(2,1)S(1)} %broadcast_in_dim.6, bf16[128]{0:T(256)(128)(2,1)} %param.23, bf16[1536]{0:T(1024)(128)(2,1)S(1)} %broadcast_in_dim.7), dimensions={0} | concatenate | bytes 8192 | tf_op jit(solution)/shard_map/concatenate | solution.py:1480
  4.0 184.6 %layer.1 = (bf16[256,1024]{1,0:T(8,128)(2,1)}, bf16[256,1024]{1,0:T(8,128)(2,1)}, bf16[128,4096]{1,0:T(8,128)(2,1)}, bf16[128,3072]{1,0:T(8,128)(2,1)}, bf16[512...) custom-call(s32[8]{0:T(128)} %lens.1, s32[8]{0:T(128)} %offs.1, bf16[256,1024]{1,0:T(8,128)(2,1)} %tok.1, ...), custom_call_target="tpu_custom_call" | custom-call | tf_op jit(solution)/shard_map/layer/pallas_call | solution.py:1431
  188.6 0.0 copy-start
  188.6 1.3 slice_bitcast_fusion.1
  189.9 1.3 slice_bitcast_fusion
  191.2 2.8 %convert_element_type.14 = f32[128,4096]{1,0:T(8,128)} convert(bf16[128,4096]{1,0:T(8,128)(2,1)} %get-tuple-element.22) | non-fusion elementwise | flops 524288 | bytes 3145728 | tf_op jit(solution)/shard_map/convert_element_type | solution.py:1493
  194.0 0.0 copy-start.1
  194.0 0.0 copy-done
  194.0 0.0 copy-start.4
  194.0 1.6 convert_element_type.15
  195.5 0.0 copy-start.3
  195.5 0.0 copy-done.1
  195.5 0.0 copy-start.2
  195.5 1.3 convert_element_type.12
  196.8 0.0 copy-done.4
  196.8 0.8 convert_element_type.13
  197.7 0.0 copy-done.3
  197.7 0.8 copy.26
  198.5 0.0 copy-done.2
  198.5 0.8 copy.27
  (2 shorter events, 0.0 us)
Async XLA Ops:
  188.6 5.4 %copy-start = (bf16[512,1024]{1,0:T(8,128)(2,1)S(1)}, bf16[512,1024]{1,0:T(8,128)(2,1)}, u32[]{:S(2)}) copy-start(bf16[512,1024]{1,0:T(8,128)(2,1)} %get-tuple-element.23) | copy-start | bytes 3145732
  194.0 1.6 copy-start.1
  194.0 2.9 %copy-start.4 = (bf16[128,1024]{1,0:T(8,128)(2,1)S(1)}, bf16[128,1024]{1,0:T(8,128)(2,1)}, u32[]{:S(2)}) copy-start(bf16[128,1024]{1,0:T(8,128)(2,1)} %get-tuple-element.21) | copy-start | bytes 786436
  195.5 2.2 %copy-start.3 = (bf16[256,1024]{1,0:T(8,128)(2,1)S(1)}, bf16[256,1024]{1,0:T(8,128)(2,1)}, u32[]{:S(2)}) copy-start(bf16[256,1024]{1,0:T(8,128)(2,1)} %get-tuple-element.37) | copy-start | bytes 1572868
  195.5 2.9 %copy-start.2 = (bf16[256,1024]{1,0:T(8,128)(2,1)S(1)}, bf16[256,1024]{1,0:T(8,128)(2,1)}, u32[]{:S(2)}) copy-start(bf16[256,1024]{1,0:T(8,128)(2,1)} %get-tuple-element.38) | copy-start | bytes 1572868
